TPU v7x, 256 devices: a whole 4x4x8 slice. The times are simulated.
256 devices in a mesh: seq: 64 (over x, z, core), head: 4 (over y).
Axes of the slice: x: 4, y: 4, z: 8, core: 2. Of those that a mesh axis runs over, the one named last changes fastest.
Arguments:
- query_rows: bfloat16 [1, 16384, 2048], P(None, 'seq', 'head'), may hold values from -28 to 28
- key_rows: bfloat16 [1, 16384, 2048], P(None, 'seq', 'head'), may hold values from -4 to 4
- value_rows: bfloat16 [1, 16384, 2048], P(None, 'seq', 'head'), may hold values from -6 to 6
- grad_out: bfloat16 [1, 16384, 2048], P(None, 'seq', 'head'), may hold values from -6 to 6
- rand_blocks: int32 [1, 16, 256, 3], P(None, 'head'), may hold values from 0 to 255, as said below
- global_pos: int32 [128], replicated, may hold values from 0 to 16383, as said below
Outputs:
- attended: bfloat16 [1, 16384, 2048], P(None, 'seq', 'head')
- grad_query: bfloat16 [1, 16384, 2048], P(None, 'seq', 'head')
- grad_key: bfloat16 [1, 16384, 2048], P(None, 'seq', 'head')
- grad_value: bfloat16 [1, 16384, 2048], P(None, 'seq', 'head')
Inputs may be any that keep to these rules, and one draw needn't show every extreme that they name: `rand_blocks`: for each run of 4 query blocks and each run of 4 heads that start at multiples of these counts, taking the one sequence and all 3 picks together, at most 1 picks name a block of any one run of 4 key blocks that starts at a multiple of 4; in each such run of query blocks and heads some run of key blocks is named exactly 1 times. `global_pos`: distinct positions; the first and the last token of the sequence are among them.
All inputs are finite; a program needn't handle non-finite values.
Results may differ from a plain program's by a relative error of at most 0.006.
The roundings to bfloat16 on the way count: a program that leaves them out, or rounds other values in their place, can miss the bound.
Values may be sent and summed in bfloat16 or wider, within the bound.
A program may use at most 64 MiB of HBM per device.

v0:
```python
import jax
import jax.numpy as jnp
from jax import lax
from jax.sharding import PartitionSpec as P

BLOCK = 64


def extended_2(value, sides, width):
    for axis, dim in sides:
        size, length = (lax.axis_size(axis), value.shape[dim])
        up = [(i, (i + 1) % size) for i in range(size - 1)]
        down = [(j, i) for i, j in up]
        last = lax.slice_in_dim(value, length - width, length, axis=dim)
        first = lax.slice_in_dim(value, 0, width, axis=dim)
        before = lax.ppermute(last, axis, up)
        after = lax.ppermute(first, axis, down)
        value = jnp.concatenate([before, value, after], axis=dim)
    return value


def body(query_rows, key_rows, value_rows, grad_out, rand_blocks, global_pos):
    batch_count, tok_local, columns = query_rows.shape
    seq_count = lax.axis_size("seq")
    seq_index = lax.axis_index("seq")
    heads_local = rand_blocks.shape[1]
    total_blocks = rand_blocks.shape[2]
    pick_count = rand_blocks.shape[3]
    head_dim = columns // heads_local
    blocks_local = tok_local // BLOCK
    score_scale = head_dim ** (-0.5)
    slot_count = batch_count * heads_local * blocks_local * pick_count
    capacity = (slot_count + seq_count - 1) // seq_count
    buffer_rows = seq_count * capacity
    f32 = jnp.float32
    bf16 = jnp.bfloat16

    def to_blocks(array):
        return array.reshape(batch_count, blocks_local, BLOCK, heads_local, head_dim).transpose(
            0, 3, 1, 2, 4
        )

    def from_blocks(array):
        return array.transpose(0, 2, 3, 1, 4).reshape(batch_count, tok_local, columns)

    def pair_blocks(array):
        return array.reshape(2, batch_count, blocks_local, BLOCK, heads_local, head_dim).transpose(
            0, 1, 4, 2, 3, 5
        )

    def global_sum(array):
        return lax.psum(array, "seq")

    key_value = jnp.stack([key_rows, value_rows])
    edge_rows = jnp.concatenate([key_value[:, :, :BLOCK], key_value[:, :, -BLOCK:]], axis=2)
    extended = extended_2(edge_rows, (("seq", 2),), BLOCK)
    padded = jnp.concatenate([extended[:, :, :BLOCK], key_value, extended[:, :, -BLOCK:]], axis=2)

    def shifted(start):
        return pair_blocks(padded[:, :, start : start + tok_local])

    window_lists = jnp.concatenate([shifted(0), shifted(BLOCK), shifted(2 * BLOCK)], axis=4)
    my_table = lax.dynamic_slice_in_dim(
        rand_blocks, seq_index * blocks_local, blocks_local, 2
    ).reshape(slot_count)
    holder = my_table // blocks_local
    holder_hot = (holder[:, None] == jnp.arange(seq_count)[None, :]).astype(jnp.int32)
    holder_rank = jnp.sum((jnp.cumsum(holder_hot, axis=0) - 1) * holder_hot, axis=1)
    position = holder * capacity + holder_rank
    requests = rand_blocks.reshape(batch_count, heads_local, seq_count, blocks_local, pick_count)
    requests = requests.transpose(2, 0, 1, 3, 4).reshape(seq_count, slot_count)
    wanted = (requests // blocks_local == seq_index).astype(jnp.int32)
    wanted_rank = jnp.cumsum(wanted, axis=1) - 1
    chosen = wanted[:, None, :] * (
        wanted_rank[:, None, :] == jnp.arange(capacity)[None, :, None]
    ).astype(jnp.int32)
    slot_live = (jnp.sum(chosen, axis=2) > 0).reshape(buffer_rows)
    slot_index = jnp.sum(chosen * jnp.arange(slot_count)[None, None, :], axis=2)
    which_batch = slot_index // (heads_local * blocks_local * pick_count)
    which_head = slot_index // (blocks_local * pick_count) % heads_local
    which_block = jnp.take_along_axis(requests, slot_index, axis=1) % blocks_local
    stacked = key_value.reshape(
        2, batch_count, blocks_local, BLOCK, heads_local, head_dim
    ).transpose(1, 2, 4, 0, 3, 5)
    outgoing = stacked[which_batch, which_block, which_head].reshape(
        buffer_rows, 2, BLOCK, head_dim
    )
    incoming = lax.all_to_all(outgoing, "seq", split_axis=0, concat_axis=0, tiled=True)
    fetched = incoming[position].reshape(
        batch_count, heads_local, blocks_local, pick_count, 2, BLOCK, head_dim
    )
    fetched = fetched.transpose(4, 0, 1, 2, 3, 5, 6).reshape(
        2, batch_count, heads_local, blocks_local, pick_count * BLOCK, head_dim
    )
    local_pos = global_pos - seq_index * tok_local
    pick_hot = (local_pos[:, None] == jnp.arange(tok_local)[None, :]).astype(bf16)
    owned_rows = jnp.einsum("gt,pbtc->pbgc", pick_hot, key_value, preferred_element_type=f32)
    shared = global_sum(owned_rows).astype(bf16)
    globals_count = shared.shape[2]
    global_kv = shared.reshape(2, batch_count, globals_count, heads_local, head_dim).transpose(
        0, 1, 3, 2, 4
    )
    global_kv = jnp.broadcast_to(
        global_kv[:, :, :, None],
        (2, batch_count, heads_local, blocks_local, globals_count, head_dim),
    )
    lists_all = jnp.concatenate([window_lists, fetched, global_kv], axis=4)
    key_lists = lists_all[0]
    value_lists = lists_all[1]
    key_count = key_lists.shape[3]
    block_ids = seq_index * blocks_local + jnp.arange(blocks_local)
    column_ids = jnp.arange(key_count)[None, :]
    middle_ok = jnp.where(
        (column_ids >= 2 * BLOCK) & (column_ids < 3 * BLOCK),
        (block_ids < total_blocks - 1)[:, None],
        True,
    )
    valid_mask = jnp.where(column_ids < BLOCK, (block_ids > 0)[:, None], middle_ok)
    query_blocks = to_blocks(query_rows)
    grad_blocks = to_blocks(grad_out)
    scores = (
        jnp.einsum("bhjqd,bhjkd->bhjqk", query_blocks, key_lists, preferred_element_type=f32)
        * score_scale
    )
    scores = jnp.where(valid_mask[None, None, :, None, :], scores, -1e30)
    row_max = jnp.max(scores, axis=-1, keepdims=True)
    log_total = row_max + jnp.log(jnp.sum(jnp.exp(scores - row_max), axis=-1, keepdims=True))
    weights = jnp.exp(scores - log_total)
    weights_b = weights.astype(bf16)
    mixed_rows = jnp.einsum(
        "bhjqk,bhjkd->bhjqd", weights_b, value_lists, preferred_element_type=f32
    )
    attended = from_blocks(mixed_rows.astype(bf16))
    row_delta = jnp.sum(grad_blocks.astype(f32) * mixed_rows, axis=-1, keepdims=True)
    grad_probs = jnp.einsum(
        "bhjqd,bhjkd->bhjqk", grad_blocks, value_lists, preferred_element_type=f32
    )
    dscore_b = (weights * (grad_probs - row_delta)).astype(bf16)
    grad_query = (
        jnp.einsum("bhjqk,bhjkd->bhjqd", dscore_b, key_lists, preferred_element_type=f32)
        * score_scale
    )

    def key_grads(lower, upper):
        key_part = (
            jnp.einsum(
                "bhjqk,bhjqd->bhjkd",
                dscore_b[..., lower:upper],
                query_blocks,
                preferred_element_type=f32,
            )
            * score_scale
        )
        value_part = jnp.einsum(
            "bhjqk,bhjqd->bhjkd",
            weights_b[..., lower:upper],
            grad_blocks,
            preferred_element_type=f32,
        )
        return jnp.stack([key_part, value_part])

    window_cols = 3 * BLOCK
    random_cols = pick_count * BLOCK
    window_grads = key_grads(0, window_cols).reshape(
        2, batch_count, heads_local, blocks_local, 3, BLOCK, head_dim
    )
    padded_grads = jnp.pad(
        window_grads[:, :, :, :, 0], ((0, 0), (0, 0), (0, 0), (0, 2), (0, 0), (0, 0))
    )
    padded_grads = padded_grads + jnp.pad(
        window_grads[:, :, :, :, 1], ((0, 0), (0, 0), (0, 0), (1, 1), (0, 0), (0, 0))
    )
    padded_grads = padded_grads + jnp.pad(
        window_grads[:, :, :, :, 2], ((0, 0), (0, 0), (0, 0), (2, 0), (0, 0), (0, 0))
    )
    own_grads = padded_grads[:, :, :, 1:-1]
    rim_grads = jnp.stack([padded_grads[:, :, :, 0], padded_grads[:, :, :, -1]], axis=3)
    returned = extended_2(rim_grads.astype(jnp.bfloat16), (("seq", 3),), 1).astype(rim_grads.dtype)
    own_grads = own_grads.at[:, :, :, 0].add(returned[:, :, :, 0])
    own_grads = own_grads.at[:, :, :, -1].add(returned[:, :, :, 3])
    global_grads = jnp.sum(key_grads(window_cols + random_cols, key_count), axis=3)
    global_grads = global_grads.transpose(0, 1, 3, 2, 4).reshape(
        2, batch_count, globals_count, columns
    )
    global_summed = global_sum(global_grads)
    inside = (local_pos >= 0) & (local_pos < tok_local)
    safe_pos = jnp.where(inside, local_pos, tok_local)
    global_local = (
        jnp.zeros((2, batch_count, tok_local, columns), f32)
        .at[:, :, safe_pos]
        .add(global_summed, mode="drop")
    )
    global_part = pair_blocks(global_local)
    target = ((which_batch * blocks_local + which_block) * heads_local + which_head).reshape(
        buffer_rows
    )
    random_grads = key_grads(window_cols, window_cols + random_cols)
    per_slot = random_grads.reshape(
        2, batch_count, heads_local, blocks_local, pick_count, BLOCK, head_dim
    )
    per_slot = per_slot.transpose(1, 2, 3, 4, 0, 5, 6).reshape(slot_count, 2, BLOCK, head_dim)
    sending = jnp.zeros((buffer_rows, 2, BLOCK, head_dim), f32).at[position].set(per_slot)
    arrived = lax.all_to_all(
        sending.astype(jnp.bfloat16), "seq", split_axis=0, concat_axis=0, tiled=True
    ).astype(sending.dtype)
    kept = jnp.where(slot_live[:, None, None, None], arrived, 0.0)
    summed = (
        jnp.zeros((batch_count * blocks_local * heads_local, 2, BLOCK, head_dim), f32)
        .at[target]
        .add(kept)
    )
    random_part = summed.reshape(
        batch_count, blocks_local, heads_local, 2, BLOCK, head_dim
    ).transpose(3, 0, 2, 1, 4, 5)
    total_grads = own_grads + random_part + global_part
    grad_key = from_blocks(total_grads[0].astype(bf16))
    grad_value = from_blocks(total_grads[1].astype(bf16))
    return (attended, from_blocks(grad_query.astype(bf16)), grad_key, grad_value)


def solution(mesh):
    return jax.shard_map(
        body,
        mesh=mesh,
        in_specs=(
            P(None, "seq", "head"),
            P(None, "seq", "head"),
            P(None, "seq", "head"),
            P(None, "seq", "head"),
            P(None, "head", None, None),
            P(),
        ),
        out_specs=(
            P(None, "seq", "head"),
            P(None, "seq", "head"),
            P(None, "seq", "head"),
            P(None, "seq", "head"),
        ),
        check_vma=False,
    )
```

profile of v0, /device:TPU:1, one launch (start us, length us, event | category | flops | bytes accessed | tf_op | source)
XLA Modules:
  0.0 616.9 jit_solution(17136765739606423861)
XLA Ops:
  7.2 1.0 stack.52
  8.3 1.0 stack.53
  9.3 1.1 reshape.1069
  11.9 0.8 gather_fusion.2
  12.8 2.2 gather_fusion
  15.0 13.1 %all-to-all-start = ((bf16[64,2,64,128]{3,2,1,0:T(8,128)(2,1)}), bf16[64,2,64,128]{3,2,1,0:T(8,128)(2,1)S(1)}, u32[]{:S(2)}, u32[]{:S(2)}) async-start(bf16[64,2,64,128]{3,2,1,0:T(8,128)(2,1)} %gather_fusion), calls=%async_computation | async-start | bytes 4194304 | tf_op jit(solution)/shard_map/all_to_all | solution.py:88
  28.4 0.9 fusion.28
  29.4 2.4 collective-permute-start.1
  31.7 3.2 collective-permute-start
  35.5 1.2 convolution_bitcast_fusion.1
  37.0 277.1 %all-reduce.7 = bf16[2,1,128,512]{2,3,0,1:T(8,128)(2,1)S(1)} all-reduce(f32[2,1,128,512]{2,3,0,1:T(8,128)} %convolution_bitcast_fusion.1), channel_id=1, replica_groups=mesh['seq'=64,'head'=4] {'seq'}, use_global_device_ids=true, to_apply=%region_4.5 | all-reduce | flops 131072 | bytes 786432 | tf_op jit(solution)/shard_map/psum | solution.py:52
  314.1 0.7 pad_maximum_fusion.6
  314.8 1.0 reshape.1082
  315.8 1.0 reshape.1078
  316.9 1.9 copy.150
  318.8 2.7 pad_maximum_fusion.2
  321.5 2.8 reshape.1153
  324.3 2.2 copy.122
  326.4 2.8 reshape.1152
  329.2 2.2 copy.118
  331.4 2.1 bitcast_dynamic-update-slice_fusion.2
  333.4 1.0 bitcast_dynamic-update-slice_fusion.1
  334.4 0.9 bitcast_dynamic-update-slice_fusion
  335.3 2.0 gather_fusion.1
  337.3 1.5 copy.132
  338.9 1.4 constant_dynamic-update-slice_fusion
  340.3 1.2 broadcast_dynamic-update-slice_fusion
  341.5 2.5 bitcast_reduce_fusion
  344.1 0.7 fusion.2
  345.2 3.4 fusion.20
  348.6 2.5 fusion
  351.1 0.7 convolution_multiply_fusion
  351.8 0.7 fusion.18
  353.2 2.5 broadcast_in_dim.119
  355.7 7.8 %scatter_fusion = f32[64,2,64,128]{3,2,1,0:T(8,128)} fusion(f32[64,2,64,128]{3,2,1,0:T(8,128)} %broadcast_in_dim.119, s32[48]{0:T(128)S(1)} %fusion.62, f32[48,2,64,128]{3,2,1,0:T(8,128)S(1)} %bitcast.280), kind=kCustom, calls=%fused_computation.3 | custom fusion | bytes 9437376 | tf_op jit(solution)/shard_map/scatter | solution.py:202
  363.6 4.1 convert_element_type.125
  367.7 10.7 %all-to-all-start.1 = ((bf16[64,2,64,128]{3,2,1,0:T(8,128)(2,1)}), bf16[64,2,64,128]{3,2,1,0:T(8,128)(2,1)}, u32[]{:S(2)}, u32[]{:S(2)}) async-start(bf16[64,2,64,128]{3,2,1,0:T(8,128)(2,1)} %convert_element_type.125), calls=%async_computation.1 | async-start | bytes 4194304 | tf_op jit(solution)/shard_map/all_to_all | solution.py:203
  378.8 0.4 convolution_multiply_fusion.1
  380.7 0.8 add_convert_fusion.1
  381.5 3.5 collective-permute-start.2
  385.0 1.9 collective-permute-start.3
  387.0 1.3 convolution_bitcast_fusion
  388.7 1.4 pad_add_fusion
  390.1 2.8 fusion.12
  392.9 0.9 maximum_reduce_fusion
  394.0 0.8 reshape.1081
  394.8 1.2 copy.137
  396.0 0.8 reshape.1084
  396.8 2.1 copy.141
  398.9 2.3 slice.213
  401.2 1.0 maximum_bitcast_fusion.1
  402.2 23.0 %collective-permute-done.2 = bf16[2,1,4,1,64,128]{5,4,0,2,3,1:T(8,128)(2,1)S(1)} collective-permute-done((bf16[2,1,4,1,64,128]{5,4,0,2,3,1:T(8,128)(2,1)}, bf16[2,1,4,1,64,128]{5,4,0,2,3,1:T(8,128)(2,1)S(1)}, u32[]{:S(2)}, u32[]{:S(2)}) %collective-permute-start.2) | collective-permute-done | bytes 131104 | tf_op jit(solution)/shard_map/ppermute | solution.py:16
  425.2 2.5 collective-permute-done.3
  427.7 0.8 fusion.30
  428.5 1.7 fusion.29
  430.2 155.0 %all-reduce.6.cloned.1.call-done = f32[2,1,128,512]{2,3,0,1:T(8,128)} async-done(((f32[2,1,128,512]{2,3,0,1:T(8,128)}), f32[2,1,128,512]{2,3,0,1:T(8,128)}) %all-reduce.6.cloned.1.call-update) | async-done | bytes 524304 | tf_op jit(solution)/shard_map/psum | solution.py:52
  585.2 1.3 copy.142
  586.7 5.9 scatter_fusion.2
  592.6 1.0 reshape.1094
  593.6 3.9 convert_select_fusion
  597.6 8.8 %scatter_fusion.1 = f32[16,2,64,128]{3,2,1,0:T(8,128)S(1)} fusion(f32[16,2,64,128]{3,2,1,0:T(8,128)S(1)} %broadcast_in_dim.116, s32[64]{0:T(128)S(1)} %fusion.63, f32[64,2,64,128]{3,2,1,0:T(8,128)} %convert_select_fusion), kind=kCustom, calls=%fused_computation.4 | custom fusion | flops 1048576 | bytes 12583168 | tf_op jit(solution)/shard_map/scatter-add | solution.py:210
  606.4 1.6 fusion.15
  608.3 0.8 reshape.1096
  609.3 0.8 reshape.1095
  (93 shorter events, 7.0 us)
Async XLA Ops:
  15.0 13.1 %copy-start.12 = (bf16[1,256,512]{2,1,0:T(8,128)(2,1)S(1)}, bf16[1,256,512]{2,1,0:T(8,128)(2,1)}, u32[]{:S(2)}) copy-start(bf16[1,256,512]{2,1,0:T(8,128)(2,1)} %param.11) | copy-start | bytes 786436
  15.0 13.3 %copy-start.13 = (bf16[1,256,512]{2,1,0:T(8,128)(2,1)S(1)}, bf16[1,256,512]{2,1,0:T(8,128)(2,1)}, u32[]{:S(2)}) copy-start(bf16[1,256,512]{2,1,0:T(8,128)(2,1)} %param.12) | copy-start | bytes 786436
  15.0 320.4 %all-to-all-start = ((bf16[64,2,64,128]{3,2,1,0:T(8,128)(2,1)}), bf16[64,2,64,128]{3,2,1,0:T(8,128)(2,1)S(1)}, u32[]{:S(2)}, u32[]{:S(2)}) async-start(bf16[64,2,64,128]{3,2,1,0:T(8,128)(2,1)} %gather_fusion), calls=%async_computation | async-start | bytes 4194304 | tf_op jit(solution)/shard_map/all_to_all | solution.py:88
  28.1 6.8 %copy-start.14 = (s32[1,4,256,3]{2,1,3,0:T(4,128)S(1)}, s32[1,4,256,3]{2,1,3,0:T(4,128)}, u32[]{:S(2)}) copy-start(s32[1,4,256,3]{2,1,3,0:T(4,128)} %param.14) | copy-start | bytes 36868
  28.1 7.4 %copy-start.15 = (s32[128]{0:T(128)S(1)}, s32[128]{0:T(128)}, u32[]{:S(2)}) copy-start(s32[128]{0:T(128)} %param.15) | copy-start | bytes 1540
  28.4 286.4 %copy-start.5 = (bf16[1,256,512]{1,2,0:T(8,128)(2,1)}, bf16[1,256,512]{1,2,0:T(8,128)(2,1)S(1)}, u32[]{:S(2)}) copy-start(bf16[1,256,512]{1,2,0:T(8,128)(2,1)S(1)} %copy.116) | copy-start | bytes 786436
  29.4 289.4 %collective-permute-start.1 = (bf16[2,1,64,512]{2,3,0,1:T(8,128)(2,1)}, bf16[2,1,64,512]{2,3,0,1:T(8,128)(2,1)}, u32[]{:S(2)}, u32[]{:S(2)}) collective-permute-start(bf16[2,1,64,512]{2,3,0,1:T(8,128)(2,1)} %get-tuple-element.41), channel_id=1, source_target_pairs={{4,0},{8,4},{12,8},{16,12},{20,16},{24,20},{28,24},{32,28},{36,32}... | collective-permute-start | bytes 393224 | tf_op jit(solution)/shard_map/ppermute | solution.py:17
  31.7 287.0 %collective-permute-start = (bf16[2,1,64,512]{2,3,0,1:T(8,128)(2,1)}, bf16[2,1,64,512]{2,3,0,1:T(8,128)(2,1)}, u32[]{:S(2)}, u32[]{:S(2)}) collective-permute-start(bf16[2,1,64,512]{2,3,0,1:T(8,128)(2,1)} %get-tuple-element.42), channel_id=1, source_target_pairs={{0,4},{4,8},{8,12},{12,16},{16,20},{20,24},{24,28},{28,32},{32,36}... | collective-permute-start | bytes 393224 | tf_op jit(solution)/shard_map/ppermute | solution.py:16
  316.9 34.2 %copy-start.2 = (bf16[1,4,64,4,128]{4,3,2,1,0:T(4,128)(2,1)}, bf16[1,4,64,4,128]{4,3,2,1,0:T(4,128)(2,1)S(1)}, u32[]{:S(2)}) copy-start(bf16[1,4,64,4,128]{4,3,2,1,0:T(4,128)(2,1)S(1)} %reshape.1078) | copy-start | bytes 786436
  331.4 3.0 copy-start.6
  338.9 1.4 copy-start.11
  345.2 6.6 %copy-start = (bf16[1,4,4,64,512]{4,3,2,1,0:T(8,128)(2,1)}, bf16[1,4,4,64,512]{4,3,2,1,0:T(8,128)(2,1)S(1)}, u32[]{:S(2)}) copy-start(bf16[1,4,4,64,512]{4,3,2,1,0:T(8,128)(2,1)S(1)} %fusion.25) | copy-start | bytes 3145732
  351.1 1.5 copy-start.7
  367.7 11.1 %copy-start.3 = (bf16[1,4,64,4,128]{4,3,2,1,0:T(4,128)(2,1)S(1)}, bf16[1,4,64,4,128]{4,3,2,1,0:T(4,128)(2,1)}, u32[]{:S(2)}) copy-start(bf16[1,4,64,4,128]{4,3,2,1,0:T(4,128)(2,1)} %copy-done.2) | copy-start | bytes 786436
  367.7 11.1 %copy-start.8 = (bf16[4,4,64,512]{3,2,1,0:T(8,128)(2,1)S(1)}, bf16[4,4,64,512]{3,2,1,0:T(8,128)(2,1)}, u32[]{:S(2)}) copy-start(bf16[4,4,64,512]{3,2,1,0:T(8,128)(2,1)} %copy-done.7) | copy-start | bytes 3145732
  367.7 225.9 %all-to-all-start.1 = ((bf16[64,2,64,128]{3,2,1,0:T(8,128)(2,1)}), bf16[64,2,64,128]{3,2,1,0:T(8,128)(2,1)}, u32[]{:S(2)}, u32[]{:S(2)}) async-start(bf16[64,2,64,128]{3,2,1,0:T(8,128)(2,1)} %convert_element_type.125), calls=%async_computation.1 | async-start | bytes 4194304 | tf_op jit(solution)/shard_map/all_to_all | solution.py:203
  378.4 1.2 copy-start.1
  378.5 206.7 %all-reduce.6.cloned.1.call-start = ((), (), s32[]{:S(2)}) async-start(), calls=%async_computation.2 | async-start | bytes 1048576 | tf_op jit(solution)/shard_map/psum | solution.py:52
  380.7 7.6 %copy-start.4 = (bf16[1,4,64,4,128]{4,3,2,1,0:T(4,128)(2,1)S(1)}, bf16[1,4,64,4,128]{4,3,2,1,0:T(4,128)(2,1)}, u32[]{:S(2)}) copy-start(bf16[1,4,64,4,128]{4,3,2,1,0:T(4,128)(2,1)} %copy-done.2) | copy-start | bytes 786436
  380.7 7.6 %copy-start.9 = (bf16[4,4,64,512]{3,2,1,0:T(8,128)(2,1)S(1)}, bf16[4,4,64,512]{3,2,1,0:T(8,128)(2,1)}, u32[]{:S(2)}) copy-start(bf16[4,4,64,512]{3,2,1,0:T(8,128)(2,1)} %copy-done.7) | copy-start | bytes 3145732
  381.5 43.7 %collective-permute-start.2 = (bf16[2,1,4,1,64,128]{5,4,0,2,3,1:T(8,128)(2,1)}, bf16[2,1,4,1,64,128]{5,4,0,2,3,1:T(8,128)(2,1)S(1)}, u32[]{:S(2)}, u32[]{:S(2)}) collective-permute-start(bf16[2,1,4,1,64,128]{5,4,0,2,3,1:T(8,128)(2,1)} %get-tuple-element.32), channel_id=1, source_target_pairs={{0,4},{4,8},{8,12},{12,16},{16,20},{20,24},{24,28},{28,32},{32,36}... | collective-permute-start | bytes 393224 | tf_op jit(solution)/shard_map/ppermute | solution.py:16
  385.0 42.7 %collective-permute-start.3 = (bf16[2,1,4,1,64,128]{5,4,0,2,3,1:T(8,128)(2,1)}, bf16[2,1,4,1,64,128]{5,4,0,2,3,1:T(8,128)(2,1)}, u32[]{:S(2)}, u32[]{:S(2)}) collective-permute-start(bf16[2,1,4,1,64,128]{5,4,0,2,3,1:T(8,128)(2,1)} %get-tuple-element.33), channel_id=1, source_target_pairs={{4,0},{8,4},{12,8},{16,12},{20,16},{24,20},{28,24},{32,28},{36,32}... | collective-permute-start | bytes 393224 | tf_op jit(solution)/shard_map/ppermute | solution.py:17
  392.9 0.9 copy-start.10
Sparse Core Ops, SparseCore 0:
  399.0 186.1 all-reduce.5
where the time goes:
time: 620 us; the launch traced here: 617 us
  blocking collectives  277 us (45%)
  waiting for transfers between devices  181 us (29%)
  local copies, waits for them, and re-layouts  55 us (9%)
  other arithmetic  38.2 us (6%)
  starting transfers between devices  35.1 us (6%)
  matrix products  16.4 us (3%)
  between operations  14.7 us (2%)
    psum x1, blocking collectives, global_sum(): return lax.psum(array, 'seq')  277 us
    psum x1, waiting for transfers between devices, global_sum(): return lax.psum(array, 'seq')  155 us
    ppermute x2, waiting for transfers between devices, extended_2(): before = lax.ppermute(last, axis, up)  23 us
    all_to_all x1, starting transfers between devices, body(): lax.all_to_all(outgoing, 'seq', split_axis=0, concat_axis=0, tiled=True)  13.1 us
  transfers between devices with their start and end apart: 7, of which 3 were waited for; matrix products, arithmetic and copies ran while one was open for 9% of the time, Pallas kernels for 0%

commit v1 on v0

v1 whole, which is shorter than its diff:
```python
import functools

import jax
import jax.numpy as jnp
from jax import lax
from jax.experimental import pallas as pl
from jax.experimental.pallas import tpu as pltpu
from jax.sharding import PartitionSpec as P

BLOCK = 64
DIM = 128
HEADS = 4
BLOCKS = 4
PICKS = 3
TOK = BLOCK * BLOCKS
COLS = HEADS * DIM
GLOB = 128
TILE = 16
GROUPS = GLOB // TILE
BF16 = jnp.bfloat16
F32 = jnp.float32
MESH = pl.DeviceIdType.MESH
VMEM = pl.BlockSpec(memory_space=pltpu.VMEM)
SMEM = pl.BlockSpec(memory_space=pltpu.SMEM)


def send_to(peer, src, dst, sems):
    return pltpu.make_async_remote_copy(
        src_ref=src,
        dst_ref=dst,
        send_sem=sems[0],
        recv_sem=sems[1],
        device_id={"seq": peer},
        device_id_type=MESH,
    )


def greet(me, size):
    barrier = pltpu.get_barrier_semaphore()

    @pl.loop(1, size)
    def _(k):
        pl.semaphore_signal(
            barrier,
            inc=1,
            device_id={"seq": lax.rem(me + k, size)},
            device_id_type=MESH,
        )

    return barrier


def exchange(me, size, barrier, edges, edge_out, tiles, part, tile, tiles_out, slots, slots_out, sems):
    edge_sems, part_sems, tile_sems, slot_sems = sems
    right, left = lax.rem(me + 1, size), lax.rem(me + size - 1, size)
    part[me] = tiles[me]
    slots_out[me] = slots[me]
    pl.semaphore_wait(barrier, size - 1)
    copies = [send_to(left, src, edge_out.at[1, at], edge_sems[i]) for i, (src, at) in enumerate(edges[0])]
    copies += [send_to(right, src, edge_out.at[0, at], edge_sems[2 + i]) for i, (src, at) in enumerate(edges[1])]
    for copy in copies:
        copy.start()

    @pl.loop(1, size)
    def _(k):
        peer = lax.rem(me + k, size)
        send_to(peer, tiles.at[peer], part.at[me], part_sems).start()

    @pl.loop(1, size)
    def _(k):
        peer = lax.rem(me + k, size)
        send_to(peer, slots.at[peer], slots_out.at[me], slot_sems).start()

    rest = pl.ds(0, size - 1)
    send_to(right, tiles.at[rest], part.at[rest], part_sems).wait()
    tile[...] = jnp.sum(part[...].astype(F32), axis=0).astype(BF16)
    tiles_out[me] = tile[...]

    @pl.loop(1, size)
    def _(k):
        peer = lax.rem(me + k, size)
        send_to(peer, tile, tiles_out.at[me], tile_sems).start()

    send_to(right, tiles.at[rest], tiles_out.at[rest], tile_sems).wait()
    for copy in copies:
        copy.wait()
    send_to(right, slots.at[rest], slots_out.at[rest], slot_sems).wait()


def sem_pairs(edge, part, tile, slot):
    edge_sems = [(edge.at[0, i], edge.at[1, i]) for i in range(4)]
    return edge_sems, (part.at[0], part.at[1]), (tile.at[0], tile.at[1]), (slot.at[0], slot.at[1])


def fetch_kernel(
    size, want, pos, key, value, slots_out, edge_out, tiles_out, stacked, slots, tiles, part, tile, *dma
):
    me = lax.axis_index("seq")
    barrier = greet(me, size)
    for j in range(BLOCKS):
        for h in range(HEADS):
            rows, cols = pl.ds(j * BLOCK, BLOCK), pl.ds(h * DIM, DIM)
            stacked[j * HEADS + h, :BLOCK] = key[rows, cols]
            stacked[j * HEADS + h, BLOCK:] = value[rows, cols]
    hot = (pos[...] - me * TOK == lax.broadcasted_iota(jnp.int32, (GLOB, TOK), 1)).astype(F32).astype(BF16)
    for c, ref in enumerate((key, value)):
        owned = jnp.dot(hot, ref[...], preferred_element_type=F32).astype(BF16)
        for g in range(GROUPS):
            for h in range(HEADS):
                tiles[g * 2 * HEADS + c * HEADS + h] = owned[g * TILE : (g + 1) * TILE, h * DIM : (h + 1) * DIM]

    @pl.loop(0, size)
    def _(k):
        slots[k] = stacked[want[k]]

    last, first = pl.ds(TOK - BLOCK, BLOCK), pl.ds(0, BLOCK)
    upper, lower = pl.ds(0, BLOCK), pl.ds(BLOCK, BLOCK)
    edges = (
        ((key.at[first], upper), (value.at[first], lower)),
        ((key.at[last], upper), (value.at[last], lower)),
    )
    exchange(me, size, barrier, edges, edge_out, tiles, part, tile, tiles_out, slots, slots_out, sem_pairs(*dma))


def return_kernel(size, edge_in, tiles, slots, edge_out, tiles_out, slots_out, part, tile, *dma):
    me = lax.axis_index("seq")
    barrier = greet(me, size)
    upper, lower = pl.ds(0, BLOCK), pl.ds(BLOCK, BLOCK)
    edges = (
        ((edge_in.at[0, upper], upper), (edge_in.at[0, lower], lower)),
        ((edge_in.at[1, upper], upper), (edge_in.at[1, lower], lower)),
    )
    exchange(me, size, barrier, edges, edge_out, tiles, part, tile, tiles_out, slots, slots_out, sem_pairs(*dma))


def dot_nt(a, b):
    return lax.dot_general(a, b, (((1,), (1,)), ((), ())), preferred_element_type=F32)


def dot_tn(a, b):
    return lax.dot_general(a, b, (((0,), (0,)), ((), ())), preferred_element_type=F32)


def dot_nn(a, b):
    return jnp.dot(a, b, preferred_element_type=F32)


def attention_kernel(
    last_device, table, query, key, value, grad, edge, tiles, slots, attended, grad_query, own_key, own_value, edge_out, tiles_out, slots_out
):
    me = table[HEADS * BLOCKS * PICKS]
    scale = DIM**-0.5
    wide = (BLOCKS + 2) * BLOCK
    query_block = lax.broadcasted_iota(jnp.int32, (TOK, wide), 0) // BLOCK
    key_block = lax.broadcasted_iota(jnp.int32, (TOK, wide), 1) // BLOCK
    low = jnp.where(me == 0, 1, 0)
    high = jnp.where(me == last_device, BLOCKS, BLOCKS + 1)
    offset = key_block - query_block
    band = (offset >= 0) & (offset <= 2) & (key_block >= low) & (key_block <= high)
    for h in range(HEADS):
        cols = pl.ds(h * DIM, DIM)
        q, g = query[:, cols], grad[:, cols]
        keys = jnp.concatenate([edge[0, :BLOCK, cols], key[:, cols], edge[1, :BLOCK, cols]], axis=0)
        values = jnp.concatenate([edge[0, BLOCK:, cols], value[:, cols], edge[1, BLOCK:, cols]], axis=0)
        global_keys = jnp.concatenate([tiles[i * 2 * HEADS + h] for i in range(GROUPS)], axis=0)
        global_values = jnp.concatenate([tiles[i * 2 * HEADS + HEADS + h] for i in range(GROUPS)], axis=0)
        at = lambda j, p: (h * BLOCKS + j) * PICKS + p
        picked_keys = [
            jnp.concatenate([slots[table[at(j, p)], :BLOCK] for p in range(PICKS)], axis=0) for j in range(BLOCKS)
        ]
        picked_values = [
            jnp.concatenate([slots[table[at(j, p)], BLOCK:] for p in range(PICKS)], axis=0) for j in range(BLOCKS)
        ]
        rows = [slice(j * BLOCK, (j + 1) * BLOCK) for j in range(BLOCKS)]
        near = jnp.where(band, dot_nt(q, keys) * scale, -1e30)
        far = jnp.concatenate([dot_nt(q[rows[j]], picked_keys[j]) for j in range(BLOCKS)], axis=0) * scale
        glob = dot_nt(q, global_keys) * scale
        row_max = jnp.maximum(
            jnp.max(near, axis=1, keepdims=True),
            jnp.maximum(jnp.max(far, axis=1, keepdims=True), jnp.max(glob, axis=1, keepdims=True)),
        )
        near, far, glob = jnp.exp(near - row_max), jnp.exp(far - row_max), jnp.exp(glob - row_max)
        total = (
            jnp.sum(near, axis=1, keepdims=True)
            + jnp.sum(far, axis=1, keepdims=True)
            + jnp.sum(glob, axis=1, keepdims=True)
        )
        inverse = 1.0 / total
        near, far, glob = near * inverse, far * inverse, glob * inverse
        near_b, far_b, glob_b = near.astype(BF16), far.astype(BF16), glob.astype(BF16)
        mixed = dot_nn(near_b, values) + dot_nn(glob_b, global_values)
        mixed += jnp.concatenate([dot_nn(far_b[rows[j]], picked_values[j]) for j in range(BLOCKS)], axis=0)
        attended[:, cols] = mixed.astype(BF16)
        delta = jnp.sum(g.astype(F32) * mixed, axis=1, keepdims=True)
        near_d = (near * (dot_nt(g, values) - delta)).astype(BF16)
        glob_d = (glob * (dot_nt(g, global_values) - delta)).astype(BF16)
        far_g = jnp.concatenate([dot_nt(g[rows[j]], picked_values[j]) for j in range(BLOCKS)], axis=0)
        far_d = (far * (far_g - delta)).astype(BF16)
        change = dot_nn(near_d, keys) + dot_nn(glob_d, global_keys)
        change += jnp.concatenate([dot_nn(far_d[rows[j]], picked_keys[j]) for j in range(BLOCKS)], axis=0)
        grad_query[:, cols] = (change * scale).astype(BF16)
        near_key = dot_tn(near_d, q) * scale
        near_value = dot_tn(near_b, g)
        own_key[:, cols] = near_key[BLOCK : BLOCK + TOK]
        own_value[:, cols] = near_value[BLOCK : BLOCK + TOK]
        edge_out[0, :BLOCK, cols] = near_key[:BLOCK].astype(BF16)
        edge_out[0, BLOCK:, cols] = near_value[:BLOCK].astype(BF16)
        edge_out[1, :BLOCK, cols] = near_key[BLOCK + TOK :].astype(BF16)
        edge_out[1, BLOCK:, cols] = near_value[BLOCK + TOK :].astype(BF16)
        glob_key = (dot_tn(glob_d, q) * scale).astype(BF16)
        glob_value = dot_tn(glob_b, g).astype(BF16)
        for i in range(GROUPS):
            tiles_out[i * 2 * HEADS + h] = glob_key[i * TILE : (i + 1) * TILE]
            tiles_out[i * 2 * HEADS + HEADS + h] = glob_value[i * TILE : (i + 1) * TILE]
        for j in range(BLOCKS):
            far_key = (dot_tn(far_d[rows[j]], q[rows[j]]) * scale).astype(BF16)
            far_value = dot_tn(far_b[rows[j]], g[rows[j]]).astype(BF16)
            for p in range(PICKS):
                slot = table[at(j, p)]
                slots_out[slot, :BLOCK] = far_key[p * BLOCK : (p + 1) * BLOCK]
                slots_out[slot, BLOCK:] = far_value[p * BLOCK : (p + 1) * BLOCK]


def collect_kernel(last_device, want, count, pos, own_key, own_value, edge, tiles, slots, grad_key, grad_value, total):
    me = count[count.shape[0] - 1]
    for j in range(BLOCKS):
        for h in range(HEADS):
            rows, cols = pl.ds(j * BLOCK, BLOCK), pl.ds(h * DIM, DIM)
            total[j * HEADS + h, :BLOCK] = own_key[rows, cols]
            total[j * HEADS + h, BLOCK:] = own_value[rows, cols]

    @pl.loop(0, slots.shape[0])
    def _(k):
        @pl.when(count[k] > 0)
        def _():
            total[want[k]] += slots[k].astype(F32)

    from_left = jnp.where(me == 0, 0.0, 1.0)
    from_right = jnp.where(me == last_device, 0.0, 1.0)
    hot = (lax.broadcasted_iota(jnp.int32, (TOK, GLOB), 0) == pos[...] - me * TOK).astype(F32).astype(BF16)
    for h in range(HEADS):
        cols = pl.ds(h * DIM, DIM)
        for c, out in enumerate((grad_key, grad_value)):
            part = pl.ds(c * BLOCK, BLOCK)
            glob = jnp.concatenate([tiles[i * 2 * HEADS + c * HEADS + h] for i in range(GROUPS)], axis=0)
            placed = dot_nn(hot, glob)
            for j in range(BLOCKS):
                whole = total[j * HEADS + h, part] + placed[j * BLOCK : (j + 1) * BLOCK]
                if j == 0:
                    whole += edge[0, part, cols].astype(F32) * from_left
                if j == BLOCKS - 1:
                    whole += edge[1, part, cols].astype(F32) * from_right
                out[pl.ds(j * BLOCK, BLOCK), cols] = whole.astype(BF16)


def body(query_rows, key_rows, value_rows, grad_out, rand_blocks, global_pos):
    size = lax.axis_size("seq")
    me = lax.axis_index("seq")
    query, key, value, grad = (a.reshape(TOK, COLS) for a in (query_rows, key_rows, value_rows, grad_out))
    picks = rand_blocks.reshape(HEADS, size, BLOCKS * PICKS)
    mine = lax.dynamic_slice_in_dim(picks, me, 1, 1).reshape(HEADS * BLOCKS * PICKS)
    table = jnp.concatenate([mine // BLOCKS, me[None]])
    named = (picks // BLOCKS == me).astype(jnp.int32)
    code = picks % BLOCKS * HEADS + jnp.arange(HEADS)[:, None, None]
    want = jnp.sum(named * code, axis=(0, 2))
    count = jnp.concatenate([jnp.sum(named, axis=(0, 2)), me[None]])

    shape = jax.ShapeDtypeStruct
    slot_shape, tile_shape, edge_shape = (size, 2 * BLOCK, DIM), (size, TILE, DIM), (2, 2 * BLOCK, COLS)
    comm_scratch = [
        pltpu.VMEM(tile_shape, BF16),
        pltpu.VMEM((TILE, DIM), BF16),
        pltpu.SemaphoreType.DMA((2, 4)),
        pltpu.SemaphoreType.DMA((2,)),
        pltpu.SemaphoreType.DMA((2,)),
        pltpu.SemaphoreType.DMA((2,)),
    ]
    slots, edge, tiles = pl.pallas_call(
        functools.partial(fetch_kernel, size),
        out_shape=[shape(slot_shape, BF16), shape(edge_shape, BF16), shape(tile_shape, BF16)],
        in_specs=[SMEM, VMEM, VMEM, VMEM],
        out_specs=[VMEM] * 3,
        scratch_shapes=[
            pltpu.VMEM((BLOCKS * HEADS, 2 * BLOCK, DIM), BF16),
            pltpu.VMEM(slot_shape, BF16),
            pltpu.VMEM(tile_shape, BF16),
            *comm_scratch,
        ],
        compiler_params=pltpu.CompilerParams(
            collective_id=0, has_side_effects=True, vmem_limit_bytes=32 << 20
        ),
        name="fetch",
    )(want, global_pos[:, None], key, value)
    wide = shape((TOK, COLS), F32)
    narrow = shape((TOK, COLS), BF16)
    attended, grad_query, own_key, own_value, edge_grads, tile_grads, slot_grads = pl.pallas_call(
        functools.partial(attention_kernel, size - 1),
        out_shape=[narrow, narrow, wide, wide, shape(edge_shape, BF16), shape(tile_shape, BF16), shape(slot_shape, BF16)],
        in_specs=[SMEM] + [VMEM] * 7,
        out_specs=[VMEM] * 7,
        compiler_params=pltpu.CompilerParams(vmem_limit_bytes=32 << 20),
        name="attention",
    )(table, query, key, value, grad, edge, tiles, slots)
    edge_back, tiles_back, slots_back = pl.pallas_call(
        functools.partial(return_kernel, size),
        out_shape=[shape(edge_shape, BF16), shape(tile_shape, BF16), shape(slot_shape, BF16)],
        in_specs=[VMEM] * 3,
        out_specs=[VMEM] * 3,
        scratch_shapes=comm_scratch,
        compiler_params=pltpu.CompilerParams(
            collective_id=1, has_side_effects=True, vmem_limit_bytes=32 << 20
        ),
        name="give_back",
    )(edge_grads, tile_grads, slot_grads)
    grad_key, grad_value = pl.pallas_call(
        functools.partial(collect_kernel, size - 1),
        out_shape=[narrow, narrow],
        in_specs=[SMEM, SMEM] + [VMEM] * 6,
        out_specs=[VMEM] * 2,
        scratch_shapes=[pltpu.VMEM((BLOCKS * HEADS, 2 * BLOCK, DIM), F32)],
        compiler_params=pltpu.CompilerParams(vmem_limit_bytes=32 << 20),
        name="collect",
    )(want, count, global_pos[None, :], own_key, own_value, edge_back, tiles_back, slots_back)
    return tuple(a.reshape(1, TOK, COLS) for a in (attended, grad_query, grad_key, grad_value))


def solution(mesh):
    rows = P(None, "seq", "head")
    return jax.shard_map(
        body,
        mesh=mesh,
        in_specs=(rows, rows, rows, rows, P(None, "head", None, None), P()),
        out_specs=(rows, rows, rows, rows),
        check_vma=False,
    )
```

time: 620 us -> 155 us (0.25)
  blocking collectives: 277 us -> 0 us
  waiting for transfers between devices: 181 us -> 0 us
  Pallas kernels: 0 us -> 149 us
  local copies, waits for them, and re-layouts: 55 us -> 4.1 us
  other arithmetic: 38.2 us -> 1.2 us
  starting transfers between devices: 35.1 us -> 0 us
  matrix products: 16.4 us -> 0 us
  between operations: 14.7 us -> 0.75 us
    psum x1 -> x0, blocking collectives: 277 us -> none  [global_sum(): return lax.psum(array, 'seq')]
    psum x1 -> x0, waiting for transfers between devices: 155 us -> none  [global_sum(): return lax.psum(array, 'seq')]
    pallas_call x0 -> x4, Pallas kernels: none -> 149 us  [the longest x1 72.8 us: body(): pl.pallas_call(functools.partial(fetch_kernel, size), out_shape=[shape(sl...]
    ppermute x4 -> x0, waiting for transfers between devices: 25.5 us -> none  [the longest x2 23 us: extended_2(): before = lax.ppermute(last, axis, up)]
    all_to_all x2 -> x0, starting transfers between devices: 23.9 us -> none  [the longest x1 13.1 us: body(): lax.all_to_all(outgoing, 'seq', split_axis=0, concat_axis=0, tiled=True)]
    reshape x17 -> x2, local copies, waits for them, and re-layouts: 19.1 us -> 0.25 us  [the longest x1 0.17 us: body(): picks = rand_blocks.reshape(HEADS, size, BLOCKS * PICKS)]
    scatter-add x4 -> x0, other arithmetic: 17.1 us -> none  [the longest x1 8.79 us: body(): summed = jnp.zeros((batch_count * blocks_local * heads_local, 2, BLOCK, h...]
    dot_general x11 -> x0, matrix products: 16.4 us -> none  [the longest x1 3.37 us: body(): jnp.einsum('bhjqk,bhjkd->bhjqd', weights_b, value_lists, preferred_elemen...]
  transfers between devices with their start and end apart: 7 -> 0, of which waited for: 3 -> 0; matrix products, arithmetic and copies ran while one was open for 9% -> 0% of each run, Pallas kernels for 0% -> 0%
where the time goes in v1:
time: 155 us
  Pallas kernels  149 us (96%)
  local copies, waits for them, and re-layouts  4.1 us (3%)
    pallas_call x1, Pallas kernels, body(): pl.pallas_call(functools.partial(fetch_kernel, size), out_shape=[shape(sl...  72.8 us
    pallas_call x1, Pallas kernels, body(): pl.pallas_call(functools.partial(return_kernel, size), out_shape=[shape(e...  66.8 us
    pallas_call x1, Pallas kernels, body(): pl.pallas_call(functools.partial(attention_kernel, size - 1), out_shape=[...  6.47 us

profile of v1, /device:TPU:1, one launch (start us, length us, event | category | flops | bytes accessed | tf_op | source)
XLA Modules:
  0.0 155.0 jit_solution(1515777149994644398)
XLA Ops:
  0.6 0.0 copy-start.4
  0.6 0.0 copy-start.1
  0.7 0.0 copy-start.3
  0.7 0.8 convert_reduce_fusion
  1.5 0.1 reduce_sum.36
  1.6 0.1 reduce_sum.37
  1.7 0.1 pad_add_fusion.1.count
  1.8 0.1 reduce_sum.24
  1.9 0.1 reduce_sum.25.want
  2.0 0.8 copy.12.pos
  2.8 0.9 copy.11
  3.7 0.2 reshape.40
  3.9 0.1 reshape.41
  4.0 0.1 pad_add_fusion.table
  4.1 0.0 copy-start
  4.1 0.9 copy-done
  5.0 0.0 copy-start.2
  5.0 0.9 copy-done.2
  6.0 72.8 %fetch.1 = (bf16[64,128,128]{2,1,0:T(8,128)(2,1)S(1)}, bf16[2,128,512]{2,1,0:T(8,128)(2,1)S(1)}, bf16[64,16,128]{2,1,0:T(8,128)(2,1)S(1)}) custom-call(s32[64]{0:T(128)S(1)} %reduce_sum.25.want, s32[128,1]{1,0:T(8,128)S(1)} %copy.12.pos, bf16[256,512]{1,0:T(8,128)(2,1)S(1)} %bitcast.13, bf16[256,512]{1,0:T(8,128)(2,1)S(1)} %bitcast.15), custom_call_target="tpu_custom_call" | custom-call | tf_op jit(solution)/shard_map/fetch/pallas_call | solution.py:278
  78.8 0.0 copy-done.4
  78.8 0.0 copy-done.1
  78.8 0.0 copy-done.3
  78.8 6.5 %attention.1 = (bf16[256,512]{1,0:T(8,128)(2,1)}, bf16[256,512]{1,0:T(8,128)(2,1)}, f32[256,512]{1,0:T(8,128)S(1)}, f32[256,512]{1,0:T(8,128)S(1)}, bf16[2,128,5...) custom-call(s32[49]{0:T(128)S(1)} %pad_add_fusion.table, ...), custom_call_target="tpu_custom_call" | custom-call | tf_op jit(solution)/shard_map/attention/pallas_call | solution.py:296
  85.3 0.0 copy-start.5
  85.3 66.8 %give_back.1 = (bf16[2,128,512]{2,1,0:T(8,128)(2,1)S(1)}, bf16[64,16,128]{2,1,0:T(8,128)(2,1)S(1)}, bf16[64,128,128]{2,1,0:T(8,128)(2,1)S(1)}) custom-call(bf16[2,128,512]{2,1,0:T(8,128)(2,1)S(1)} %get-tuple-element.26.edge_in, bf16[64,16,128]{2,1,0:T(8,128)(2,1)S(1)} %get-tuple-element.27.tiles, bf16[64,128,128]{2,1,0:T(8,128)(2,1)S(1)} %get-tuple-element.28.slots), custom_call_target="tpu_custom_call" | custom-call | tf_op jit(solution)/shard_map/give_back/pallas_call | solution.py:304
  152.1 0.0 copy-done.5
  152.1 2.9 %collect.1 = (bf16[256,512]{1,0:T(8,128)(2,1)}, bf16[256,512]{1,0:T(8,128)(2,1)}) custom-call(s32[64]{0:T(128)S(1)} %reduce_sum.25.want, s32[65]{0:T(128)S(1)} %pad_add_fusion.1.count, s32[1,128]{1,0:T(1,128)S(1)} %bitcast.20, f32[256,512]{1,0:T(8,128)S(1)} %get-tuple-element.24.own_key, f32[256,512]{1,0:T(8,128)S(1)} %get-tuple-element.25.own_value, ...), custom_call_target="tpu_custom_call" | custom-call | tf_op jit(solution)/shard_map/collect/pallas_call | solution.py:315
  (2 shorter events, 0.0 us)
Async XLA Ops:
  0.6 78.1 %copy-start.4 = (bf16[1,256,512]{2,1,0:T(8,128)(2,1)S(1)}, bf16[1,256,512]{2,1,0:T(8,128)(2,1)}, u32[]{:S(2)}) copy-start(bf16[1,256,512]{2,1,0:T(8,128)(2,1)} %param.9) | copy-start | bytes 786436
  0.6 78.1 %copy-start.1 = (bf16[1,256,512]{2,1,0:T(8,128)(2,1)S(1)}, bf16[1,256,512]{2,1,0:T(8,128)(2,1)}, u32[]{:S(2)}) copy-start(bf16[1,256,512]{2,1,0:T(8,128)(2,1)} %param.7) | copy-start | bytes 786436
  0.7 78.1 %copy-start.3 = (bf16[1,256,512]{2,1,0:T(8,128)(2,1)S(1)}, bf16[1,256,512]{2,1,0:T(8,128)(2,1)}, u32[]{:S(2)}) copy-start(bf16[1,256,512]{2,1,0:T(8,128)(2,1)} %param.6) | copy-start | bytes 786436
  4.1 1.0 copy-start
  5.0 0.9 copy-start.2
  85.3 66.8 %copy-start.5 = (s32[128]{0:T(128)S(1)}, s32[128]{0:T(128)}, u32[]{:S(2)}) copy-start(s32[128]{0:T(128)} %param.11) | copy-start | bytes 1540

commit v2 on v1

v2 whole, which is shorter than its diff:
```python
import functools

import jax
import jax.numpy as jnp
from jax import lax
from jax.experimental import pallas as pl
from jax.experimental.pallas import tpu as pltpu
from jax.sharding import PartitionSpec as P

BLOCK = 64
DIM = 128
HEADS = 4
BLOCKS = 4
PICKS = 3
TOK = BLOCK * BLOCKS
COLS = HEADS * DIM
GLOB = 128
TILE = 16
GROUPS = GLOB // TILE
SEQ = 64
RING = 8
NPICK = HEADS * BLOCKS * PICKS
WIDE = (BLOCKS + 2) * BLOCK
FAR = PICKS * BLOCK
SCALE = DIM**-0.5
CHUNKS = (1, 9, 17, 25, SEQ)
BF16 = jnp.bfloat16
F32 = jnp.float32
MESH = pl.DeviceIdType.MESH
VMEM = pl.BlockSpec(memory_space=pltpu.VMEM)
SMEM = pl.BlockSpec(memory_space=pltpu.SMEM)
ANY = pl.BlockSpec(memory_space=pl.ANY)
UPPER, LOWER = pl.ds(0, BLOCK), pl.ds(BLOCK, BLOCK)


def send_to(peer, src, dst, sems):
    return pltpu.make_async_remote_copy(
        src_ref=src,
        dst_ref=dst,
        send_sem=sems.at[0],
        recv_sem=sems.at[1],
        device_id={"seq": peer},
        device_id_type=MESH,
    )


def dot_nt(a, b):
    return lax.dot_general(a, b, (((1,), (1,)), ((), ())), preferred_element_type=F32)


def dot_tn(a, b):
    return lax.dot_general(a, b, (((0,), (0,)), ((), ())), preferred_element_type=F32)


def dot_nn(a, b):
    return jnp.dot(a, b, preferred_element_type=F32)


class Tiles:
    def __init__(self, me, tiles, part, middle, piece, row, out, sems):
        self.z, self.xc = me // 2 % RING, me // (2 * RING) * 2 + me % 2
        self.tiles, self.part, self.middle, self.piece, self.row, self.out = tiles, part, middle, piece, row, out
        self.sems = sems

    def along_xc(self, k):
        other = lax.rem(self.xc + k, RING)
        return other, (other // 2 * RING + self.z) * 2 + other % 2

    def along_z(self, k):
        other = lax.rem(self.z + k, RING)
        return other, (self.xc // 2 * RING + other) * 2 + self.xc % 2

    def start_first(self):
        for k in range(1, RING):
            other, peer = self.along_xc(k)
            send_to(peer, self.tiles.at[other], self.part.at[self.xc], self.sems.at[0]).start()
        self.part[self.xc] = self.tiles[self.xc]

    def start_second(self):
        rest = pl.ds(0, RING - 1)
        send_to(self.along_xc(1)[1], self.tiles.at[rest], self.part.at[rest], self.sems.at[0]).wait()
        self.middle[...] = jnp.sum(self.part[...].astype(F32), axis=0).astype(BF16)
        for k in range(1, RING):
            other, peer = self.along_z(k)
            send_to(peer, self.middle.at[other], self.piece.at[self.z], self.sems.at[1]).start()
        self.piece[self.z] = self.middle[self.z]

    def start_third(self):
        rest = pl.ds(0, RING - 1)
        send_to(self.along_z(1)[1], self.middle.at[rest], self.piece.at[rest], self.sems.at[1]).wait()
        self.row[self.z] = jnp.sum(self.piece[...].astype(F32), axis=0).astype(BF16)
        for k in range(1, RING):
            _, peer = self.along_z(k)
            send_to(peer, self.row.at[self.z], self.row.at[self.z], self.sems.at[2]).start()

    def start_fourth(self):
        rest = pl.ds(0, RING - 1)
        send_to(self.along_z(1)[1], self.row.at[rest], self.row.at[rest], self.sems.at[2]).wait()
        for k in range(1, RING):
            _, peer = self.along_xc(k)
            send_to(peer, self.row, self.out.at[self.xc], self.sems.at[3]).start()
        self.out[self.xc] = self.row[...]

    def finish(self):
        rest = pl.ds(0, RING - 1)
        send_to(self.along_xc(1)[1], self.tiles.at[rest], self.out.at[rest], self.sems.at[3]).wait()


def main_kernel(
    tables, pos, query_hbm, key_hbm, value_hbm, grad_hbm,
    attended, grad_query, own_key, own_value, edge_back, tiles_back, slots_back,
    query, key, value, grad, stacked, slots_out, slots, edge, tiles_in, part, middle, piece, row, tiles,
    near_s, near_g, glob_s, glob_g, near_p, near_d, glob_d, glob_p, far_s, picked,
    edge_grads, back_in, back_part, back_middle, back_piece, back_row, back_out,
    local_sems, edge_sems, tile_sems, slot_sems, edge_back_sems, tile_back_sems, slot_back_sems,
):
    me = lax.axis_index("seq")
    right, left = lax.rem(me + 1, SEQ), lax.rem(me + SEQ - 1, SEQ)
    want = lambda k: tables[k]
    given = lambda k: tables[SEQ + k]
    holder = lambda h, j, p: tables[2 * SEQ + (h * BLOCKS + j) * PICKS + p]
    barrier = pltpu.get_barrier_semaphore()

    @pl.loop(1, SEQ)
    def _(k):
        pl.semaphore_signal(barrier, inc=1, device_id={"seq": lax.rem(me + k, SEQ)}, device_id_type=MESH)

    loads = [
        pltpu.make_async_copy(src, dst, local_sems.at[i])
        for i, (src, dst) in enumerate(((key_hbm, key), (value_hbm, value), (query_hbm, query), (grad_hbm, grad)))
    ]
    for copy in loads:
        copy.start()
    loads[0].wait()
    loads[1].wait()

    for j in range(BLOCKS):
        for h in range(HEADS):
            rows, cols = pl.ds(j * BLOCK, BLOCK), pl.ds(h * DIM, DIM)
            stacked[j * HEADS + h, UPPER] = key[rows, cols]
            stacked[j * HEADS + h, LOWER] = value[rows, cols]
    hot = (lax.broadcasted_iota(jnp.int32, (TOK, GLOB), 0) == pos[...] - me * TOK).astype(F32).astype(BF16)
    for c, ref in enumerate((key, value)):
        owned = dot_tn(hot, ref[...]).astype(BF16)
        for g in range(GROUPS):
            for h in range(HEADS):
                tiles_in[g, c * HEADS + h] = owned[g * TILE : (g + 1) * TILE, h * DIM : (h + 1) * DIM]

    def fill_slot(k):
        slots_out[k] = stacked[want(k)]

    @pl.loop(0, SEQ)
    def _(k):
        fill_slot(k)

    slots[me] = slots_out[me]

    def send_slots(chunk):
        @pl.loop(CHUNKS[chunk], CHUNKS[chunk + 1])
        def _(k):
            peer = lax.rem(me + k, SEQ)
            send_to(peer, slots_out.at[peer], slots.at[me], slot_sems).start()

    pl.semaphore_wait(barrier, SEQ - 1)
    last, first = pl.ds(TOK - BLOCK, BLOCK), pl.ds(0, BLOCK)
    edges = [
        send_to(left, key.at[first], edge.at[1, UPPER], edge_sems.at[0]),
        send_to(left, value.at[first], edge.at[1, LOWER], edge_sems.at[1]),
        send_to(right, key.at[last], edge.at[0, UPPER], edge_sems.at[2]),
        send_to(right, value.at[last], edge.at[0, LOWER], edge_sems.at[3]),
    ]
    shared = Tiles(me, tiles_in, part, middle, piece, row, tiles, tile_sems)
    shared.start_first()
    for copy in edges:
        copy.start()
    send_slots(0)
    shared.start_second()
    send_slots(1)
    shared.start_third()
    send_slots(2)
    shared.start_fourth()
    send_slots(3)

    loads[2].wait()
    loads[3].wait()
    for copy in edges:
        copy.wait()
    query_block = lax.broadcasted_iota(jnp.int32, (TOK, WIDE), 0) // BLOCK
    key_block = lax.broadcasted_iota(jnp.int32, (TOK, WIDE), 1) // BLOCK
    low = jnp.where(me == 0, 1, 0)
    high = jnp.where(me == SEQ - 1, BLOCKS, BLOCKS + 1)
    offset = key_block - query_block
    band = (offset >= 0) & (offset <= 2) & (key_block >= low) & (key_block <= high)

    def near_keys(cols):
        return jnp.concatenate([edge[0, UPPER, cols], key[:, cols], edge[1, UPPER, cols]], axis=0)

    def near_values(cols):
        return jnp.concatenate([edge[0, LOWER, cols], value[:, cols], edge[1, LOWER, cols]], axis=0)

    def glob_keys(h):
        return jnp.concatenate([tiles[g, h] for g in range(GROUPS)], axis=0)

    def glob_values(h):
        return jnp.concatenate([tiles[g, HEADS + h] for g in range(GROUPS)], axis=0)

    for h in range(HEADS):
        cols = pl.ds(h * DIM, DIM)
        near_s[h] = jnp.where(band, dot_nt(query[:, cols], near_keys(cols)) * SCALE, -1e30)
        near_g[h] = dot_nt(grad[:, cols], near_values(cols))
    shared.finish()
    for h in range(HEADS):
        cols = pl.ds(h * DIM, DIM)
        glob_s[h] = dot_nt(query[:, cols], glob_keys(h)) * SCALE
        glob_g[h] = dot_nt(grad[:, cols], glob_values(h))
    rest = pl.ds(0, SEQ - 1)
    send_to(right, slots_out.at[rest], slots.at[rest], slot_sems).wait()

    block_rows = [slice(j * BLOCK, (j + 1) * BLOCK) for j in range(BLOCKS)]
    picked[NPICK] = jnp.zeros((2 * BLOCK, DIM), BF16)
    for h in range(HEADS):
        cols = pl.ds(h * DIM, DIM)
        q, g = query[:, cols], grad[:, cols]
        keys = [jnp.concatenate([slots[holder(h, j, p), UPPER] for p in range(PICKS)], axis=0) for j in range(BLOCKS)]
        values = [jnp.concatenate([slots[holder(h, j, p), LOWER] for p in range(PICKS)], axis=0) for j in range(BLOCKS)]
        far = jnp.concatenate([dot_nt(q[block_rows[j]], keys[j]) for j in range(BLOCKS)], axis=0) * SCALE
        near, glob = near_s[h], glob_s[h]
        row_max = jnp.maximum(
            jnp.max(near, axis=1, keepdims=True),
            jnp.maximum(jnp.max(far, axis=1, keepdims=True), jnp.max(glob, axis=1, keepdims=True)),
        )
        near, far, glob = jnp.exp(near - row_max), jnp.exp(far - row_max), jnp.exp(glob - row_max)
        total = (
            jnp.sum(near, axis=1, keepdims=True)
            + jnp.sum(far, axis=1, keepdims=True)
            + jnp.sum(glob, axis=1, keepdims=True)
        )
        inverse = 1.0 / total
        near, far, glob = near * inverse, far * inverse, glob * inverse
        near_b, far_b, glob_b = near.astype(BF16), far.astype(BF16), glob.astype(BF16)
        mixed = dot_nn(near_b, near_values(cols)) + dot_nn(glob_b, glob_values(h))
        mixed += jnp.concatenate([dot_nn(far_b[block_rows[j]], values[j]) for j in range(BLOCKS)], axis=0)
        attended[:, cols] = mixed.astype(BF16)
        delta = jnp.sum(g.astype(F32) * mixed, axis=1, keepdims=True)
        far_g = jnp.concatenate([dot_nt(g[block_rows[j]], values[j]) for j in range(BLOCKS)], axis=0)
        far_d = (far * (far_g - delta)).astype(BF16)
        for j in range(BLOCKS):
            far_key = (dot_tn(far_d[block_rows[j]], q[block_rows[j]]) * SCALE).astype(BF16)
            far_value = dot_tn(far_b[block_rows[j]], g[block_rows[j]]).astype(BF16)
            for p in range(PICKS):
                at = (h * BLOCKS + j) * PICKS + p
                picked[at, UPPER] = far_key[p * BLOCK : (p + 1) * BLOCK]
                picked[at, LOWER] = far_value[p * BLOCK : (p + 1) * BLOCK]
        far_s[h] = jnp.concatenate([dot_nn(far_d[block_rows[j]], keys[j]) for j in range(BLOCKS)], axis=0)
        near_p[h] = near_b
        glob_p[h] = glob_b
        near_d[h] = (near * (near_g[h] - delta)).astype(BF16)
        glob_d[h] = (glob * (glob_g[h] - delta)).astype(BF16)

    def return_slots(chunk):
        @pl.loop(CHUNKS[chunk], CHUNKS[chunk + 1])
        def _(k):
            peer = lax.rem(me + k, SEQ)
            slots_out[peer] = picked[given(peer)]
            send_to(peer, slots_out.at[peer], slots_back.at[me], slot_back_sems).start()

    for h in range(HEADS):
        cols = pl.ds(h * DIM, DIM)
        glob_key = (dot_tn(glob_d[h], query[:, cols]) * SCALE).astype(BF16)
        glob_value = dot_tn(glob_p[h], grad[:, cols]).astype(BF16)
        for g in range(GROUPS):
            back_in[g, h] = glob_key[g * TILE : (g + 1) * TILE]
            back_in[g, HEADS + h] = glob_value[g * TILE : (g + 1) * TILE]
    summed = Tiles(me, back_in, back_part, back_middle, back_piece, back_row, back_out, tile_back_sems)
    summed.start_first()
    return_slots(0)
    slots_back[me] = picked[given(me)]
    for h in range(HEADS):
        cols = pl.ds(h * DIM, DIM)
        q, g = query[:, cols], grad[:, cols]
        near_key = dot_tn(near_d[h], q) * SCALE
        near_value = dot_tn(near_p[h], g)
        own_key[:, cols] = near_key[BLOCK : BLOCK + TOK]
        own_value[:, cols] = near_value[BLOCK : BLOCK + TOK]
        edge_grads[0, UPPER, cols] = near_key[:BLOCK].astype(BF16)
        edge_grads[0, LOWER, cols] = near_value[:BLOCK].astype(BF16)
        edge_grads[1, UPPER, cols] = near_key[BLOCK + TOK :].astype(BF16)
        edge_grads[1, LOWER, cols] = near_value[BLOCK + TOK :].astype(BF16)
    edges = [
        send_to(left, edge_grads.at[0], edge_back.at[1], edge_back_sems.at[0]),
        send_to(right, edge_grads.at[1], edge_back.at[0], edge_back_sems.at[1]),
    ]
    for copy in edges:
        copy.start()
    summed.start_second()
    return_slots(1)
    summed.start_third()
    return_slots(2)
    summed.start_fourth()
    return_slots(3)
    for h in range(HEADS):
        cols = pl.ds(h * DIM, DIM)
        change = dot_nn(near_d[h], near_keys(cols)) + dot_nn(glob_d[h], glob_keys(h)) + far_s[h]
        grad_query[:, cols] = (change * SCALE).astype(BF16)
    summed.finish()
    tiles_back[...] = back_out[...]
    for copy in edges:
        copy.wait()
    send_to(right, slots_out.at[rest], slots_back.at[rest], slot_back_sems).wait()


def collect_kernel(tables, pos, own_key, own_value, edge, tiles, slots, grad_key, grad_value, total):
    me = tables[2 * SEQ + NPICK]
    for j in range(BLOCKS):
        for h in range(HEADS):
            rows, cols = pl.ds(j * BLOCK, BLOCK), pl.ds(h * DIM, DIM)
            total[j * HEADS + h, UPPER] = own_key[rows, cols]
            total[j * HEADS + h, LOWER] = own_value[rows, cols]

    @pl.loop(0, SEQ)
    def _(k):
        total[tables[k]] += slots[k].astype(F32)

    from_left = jnp.where(me == 0, 0.0, 1.0)
    from_right = jnp.where(me == SEQ - 1, 0.0, 1.0)
    hot = (lax.broadcasted_iota(jnp.int32, (TOK, GLOB), 0) == pos[...] - me * TOK).astype(F32).astype(BF16)
    for h in range(HEADS):
        cols = pl.ds(h * DIM, DIM)
        for c, out in enumerate((grad_key, grad_value)):
            part = pl.ds(c * BLOCK, BLOCK)
            glob = jnp.concatenate([tiles[g, c * HEADS + h] for g in range(GROUPS)], axis=0)
            placed = dot_nn(hot, glob)
            for j in range(BLOCKS):
                whole = total[j * HEADS + h, part] + placed[j * BLOCK : (j + 1) * BLOCK]
                if j == 0:
                    whole += edge[0, part, cols].astype(F32) * from_left
                if j == BLOCKS - 1:
                    whole += edge[1, part, cols].astype(F32) * from_right
                out[pl.ds(j * BLOCK, BLOCK), cols] = whole.astype(BF16)


def make_tables(rand_blocks, me):
    picks = rand_blocks.reshape(HEADS, SEQ, BLOCKS * PICKS)
    holders = picks // BLOCKS
    code = picks % BLOCKS * HEADS + jnp.arange(HEADS)[:, None, None]
    want = jnp.sum(jnp.where(holders == me, code, 0), axis=(0, 2))
    mine = lax.dynamic_slice_in_dim(holders, me, 1, 1).reshape(NPICK)
    index = jnp.arange(NPICK)[None, :] - NPICK
    given = NPICK + jnp.sum(jnp.where(mine[None, :] == jnp.arange(SEQ)[:, None], index, 0), axis=1)
    return jnp.concatenate([want, given, mine, me[None]])


def body(query_rows, key_rows, value_rows, grad_out, rand_blocks, global_pos):
    me = lax.axis_index("seq")
    arrays = [a.reshape(TOK, COLS) for a in (query_rows, key_rows, value_rows, grad_out)]
    tables = make_tables(rand_blocks, me)
    pos = global_pos[None, :]
    shape = jax.ShapeDtypeStruct
    slot_shape, edge_shape = (SEQ, 2 * BLOCK, DIM), (2, 2 * BLOCK, COLS)
    grid_shape, row_shape = (RING, RING, TILE, DIM), (RING, TILE, DIM)
    wide, narrow = shape((TOK, COLS), F32), shape((TOK, COLS), BF16)
    bf16 = lambda dims: pltpu.VMEM(dims, BF16)
    f32 = lambda dims: pltpu.VMEM(dims, F32)
    dma = pltpu.SemaphoreType.DMA
    tile_scratch = [bf16(grid_shape), bf16(grid_shape), bf16(row_shape), bf16(row_shape), bf16(row_shape), bf16(grid_shape)]
    attended, grad_query, own_key, own_value, edge, tiles, slots = pl.pallas_call(
        main_kernel,
        out_shape=[narrow, narrow, wide, wide, shape(edge_shape, BF16), shape(grid_shape, BF16), shape(slot_shape, BF16)],
        in_specs=[SMEM, VMEM, ANY, ANY, ANY, ANY],
        out_specs=[VMEM] * 7,
        scratch_shapes=[
            *[bf16((TOK, COLS))] * 4,
            bf16((BLOCKS * HEADS, 2 * BLOCK, DIM)),
            bf16(slot_shape),
            bf16(slot_shape),
            bf16(edge_shape),
            *tile_scratch,
            f32((HEADS, TOK, WIDE)),
            f32((HEADS, TOK, WIDE)),
            f32((HEADS, TOK, GLOB)),
            f32((HEADS, TOK, GLOB)),
            bf16((HEADS, TOK, WIDE)),
            bf16((HEADS, TOK, WIDE)),
            bf16((HEADS, TOK, GLOB)),
            bf16((HEADS, TOK, GLOB)),
            f32((HEADS, TOK, DIM)),
            bf16((NPICK + 1, 2 * BLOCK, DIM)),
            bf16(edge_shape),
            *tile_scratch,
            dma((4,)),
            dma((4, 2)),
            dma((4, 2)),
            dma((2,)),
            dma((2, 2)),
            dma((4, 2)),
            dma((2,)),
        ],
        compiler_params=pltpu.CompilerParams(
            collective_id=0, has_side_effects=True, vmem_limit_bytes=48 << 20
        ),
        name="attend",
    )(tables, pos, *arrays)
    grad_key, grad_value = pl.pallas_call(
        collect_kernel,
        out_shape=[narrow, narrow],
        in_specs=[SMEM] + [VMEM] * 6,
        out_specs=[VMEM] * 2,
        scratch_shapes=[f32((BLOCKS * HEADS, 2 * BLOCK, DIM))],
        compiler_params=pltpu.CompilerParams(vmem_limit_bytes=32 << 20),
        name="collect",
    )(tables, pos, own_key, own_value, edge, tiles, slots)
    return tuple(a.reshape(1, TOK, COLS) for a in (attended, grad_query, grad_key, grad_value))


def solution(mesh):
    rows = P(None, "seq", "head")
    return jax.shard_map(
        body,
        mesh=mesh,
        in_specs=(rows, rows, rows, rows, P(None, "head", None, None), P()),
        out_specs=(rows, rows, rows, rows),
        check_vma=False,
    )
```

time: 155 us -> 141 us (0.910)
  Pallas kernels: 149 us -> 132 us
  local copies, waits for them, and re-layouts: 4.1 us -> 7.15 us
    pallas_call x4 -> x2, Pallas kernels: 149 us -> 132 us  [the longest x1 130 us: body(): pl.pallas_call(main_kernel, out_shape=[narrow, narrow, wide, wide, shape(...]
    unnamed x13, local copies, waits for them, and re-layouts: 2.84 us -> 6.79 us
where the time goes in v2:
time: 141 us
  Pallas kernels  132 us (94%)
  local copies, waits for them, and re-layouts  7.15 us (5%)
    pallas_call x1, Pallas kernels, body(): pl.pallas_call(main_kernel, out_shape=[narrow, narrow, wide, wide, shape(...  130 us
    unnamed x13, local copies, waits for them, and re-layouts  6.79 us

profile of v2, /device:TPU:1, one launch (start us, length us, event | category | flops | bytes accessed | tf_op | source)
XLA Modules:
  0.0 141.1 jit_solution(101378360868206345)
XLA Ops:
  0.6 0.8 fusion.4
  1.4 0.1 reduce_sum.26
  1.5 0.1 reduce_sum.27
  1.6 0.9 copy.11
  2.6 0.2 reshape.43
  2.8 0.1 eq.26
  2.9 0.1 select_reduce_fusion
  3.0 0.1 pad_add_fusion.tables
  3.1 0.0 copy-start
  3.1 1.0 copy-done
  4.1 0.0 copy-start.1
  4.1 0.9 copy-done.1
  5.0 0.0 copy-start.2
  5.0 0.9 copy-done.2
  6.0 0.0 copy-start.3
  6.0 0.9 copy-done.3
  6.9 0.0 copy-start.4
  6.9 0.7 copy-done.4
  7.6 129.7 %attend.1 = (bf16[256,512]{1,0:T(8,128)(2,1)S(1)}, bf16[256,512]{1,0:T(8,128)(2,1)S(1)}, f32[256,512]{1,0:T(8,128)S(1)}, f32[256,512]{1,0:T(8,128)S(1)}, bf16[2,...) custom-call(s32[177]{0:T(256)S(1)} %pad_add_fusion.tables, ...), custom_call_target="tpu_custom_call" | custom-call | tf_op jit(solution)/shard_map/attend/pallas_call | solution.py:366
  137.3 2.4 %collect.1 = (bf16[256,512]{1,0:T(8,128)(2,1)}, bf16[256,512]{1,0:T(8,128)(2,1)}) custom-call(s32[177]{0:T(256)S(1)} %pad_add_fusion.tables, s32[1,128]{1,0:T(1,128)S(1)} %bitcast.19, f32[256,512]{1,0:T(8,128)S(1)} %get-tuple-element.15.own_key, f32[256,512]{1,0:T(8,128)S(1)} %get-tuple-element.16.own_value, ...), custom_call_target="tpu_custom_call" | custom-call | tf_op jit(solution)/shard_map/collect/pallas_call | solution.py:403
  139.7 0.7 copy.14
  140.4 0.7 copy.15
  (5 shorter events, 0.1 us)
Async XLA Ops:
  3.1 1.0 copy-start
  4.1 0.9 copy-start.1
  5.0 0.9 copy-start.2
  6.0 0.9 copy-start.3
  6.9 0.7 copy-start.4

commit v3 on v2

--- a/solution.py
+++ b/solution.py
@@ -23,7 +23,9 @@
 WIDE = (BLOCKS + 2) * BLOCK
 FAR = PICKS * BLOCK
 SCALE = DIM**-0.5
-CHUNKS = (1, 9, 17, 25, SEQ)
+CHUNKS = (1, 21, 33, 45, SEQ)
+EARLY = 5
+MINE = 1
 BF16 = jnp.bfloat16
 F32 = jnp.float32
 MESH = pl.DeviceIdType.MESH
@@ -56,6 +58,13 @@
     return jnp.dot(a, b, preferred_element_type=F32)
 
 
+def named_by(table, device):
+    at = device * BLOCKS
+    return jnp.maximum(
+        jnp.maximum(table[0, at], table[0, at + 1]), jnp.maximum(table[0, at + 2], table[0, at + 3])
+    )
+
+
 class Tiles:
     def __init__(self, me, tiles, part, middle, piece, row, out, sems):
         self.z, self.xc = me // 2 % RING, me // (2 * RING) * 2 + me % 2
@@ -107,32 +116,64 @@
 
 
 def main_kernel(
-    tables, pos, query_hbm, key_hbm, value_hbm, grad_hbm,
-    attended, grad_query, own_key, own_value, edge_back, tiles_back, slots_back,
-    query, key, value, grad, stacked, slots_out, slots, edge, tiles_in, part, middle, piece, row, tiles,
-    near_s, near_g, glob_s, glob_g, near_p, near_d, glob_d, glob_p, far_s, picked,
+    query_hbm, key_hbm, value_hbm, grad_hbm, rand_hbm, pos_hbm,
+    attended, grad_query, own_key, own_value, edge_back, tiles_back, slots_back, table,
+    rand, rand_smem, pos, table_smem, given_vmem, given_smem, query, key, value, grad, stacked, slots_out, slots, edge, tiles_in, part, middle, piece, row, tiles,
+    near_s, near_g, glob_s, glob_g, near_p, near_d, glob_d, glob_p, far_d, row_max, row_sum, picked,
     edge_grads, back_in, back_part, back_middle, back_piece, back_row, back_out,
     local_sems, edge_sems, tile_sems, slot_sems, edge_back_sems, tile_back_sems, slot_back_sems,
 ):
     me = lax.axis_index("seq")
     right, left = lax.rem(me + 1, SEQ), lax.rem(me + SEQ - 1, SEQ)
-    want = lambda k: tables[k]
-    given = lambda k: tables[SEQ + k]
-    holder = lambda h, j, p: tables[2 * SEQ + (h * BLOCKS + j) * PICKS + p]
     barrier = pltpu.get_barrier_semaphore()
+    loads = [
+        pltpu.make_async_copy(src, dst, local_sems.at[i])
+        for i, (src, dst) in enumerate(
+            (
+                (rand_hbm, rand),
+                (rand_hbm, rand_smem),
+                (pos_hbm, pos),
+                (key_hbm, key),
+                (value_hbm, value),
+                (query_hbm, query),
+                (grad_hbm, grad),
+            )
+        )
+    ]
+    for copy in loads:
+        copy.start()
 
     @pl.loop(1, SEQ)
     def _(k):
         pl.semaphore_signal(barrier, inc=1, device_id={"seq": lax.rem(me + k, SEQ)}, device_id_type=MESH)
 
-    loads = [
-        pltpu.make_async_copy(src, dst, local_sems.at[i])
-        for i, (src, dst) in enumerate(((key_hbm, key), (value_hbm, value), (query_hbm, query), (grad_hbm, grad)))
+    for copy in loads[:5]:
+        copy.wait()
+
+    asked = jnp.zeros((HEADS, SEQ * BLOCKS), jnp.int32)
+    for p in range(PICKS):
+        names = rand[p]
+        code = (names & (BLOCKS - 1)) * HEADS + lax.broadcasted_iota(jnp.int32, names.shape, 0)
+        asked = jnp.maximum(asked, jnp.where(names >> 2 == me, code, 0))
+    asked = jnp.max(asked, axis=0, keepdims=True)
+    line = lax.broadcasted_iota(jnp.int32, (8, SEQ * BLOCKS), 0)
+    table[...] = jnp.where(line == MINE, me, asked)
+    holder = lambda h, j, p: rand_smem[p, h, me * BLOCKS + j] >> 2
+    lane = lax.broadcasted_iota(jnp.int32, (8, DIM), 1)
+    found = jnp.full((8, DIM), NPICK, jnp.int32)
+    for h in range(HEADS):
+        for j in range(BLOCKS):
+            for p in range(PICKS):
+                found = jnp.where(lane == holder(h, j, p), (h * BLOCKS + j) * PICKS + p, found)
+    given_vmem[...] = found
+    copies = [
+        pltpu.make_async_copy(table, table_smem, local_sems.at[7]),
+        pltpu.make_async_copy(given_vmem, given_smem, local_sems.at[8]),
     ]
-    for copy in loads:
+    for copy in copies:
         copy.start()
-    loads[0].wait()
-    loads[1].wait()
+    given = lambda k: given_smem[0, k]
+    want = lambda k: named_by(table_smem, k)
 
     for j in range(BLOCKS):
         for h in range(HEADS):
@@ -146,12 +187,12 @@
             for h in range(HEADS):
                 tiles_in[g, c * HEADS + h] = owned[g * TILE : (g + 1) * TILE, h * DIM : (h + 1) * DIM]
 
-    def fill_slot(k):
-        slots_out[k] = stacked[want(k)]
+    for copy in copies:
+        copy.wait()
 
     @pl.loop(0, SEQ)
     def _(k):
-        fill_slot(k)
+        slots_out[k] = stacked[want(k)]
 
     slots[me] = slots_out[me]
 
@@ -181,8 +222,8 @@
     shared.start_fourth()
     send_slots(3)
 
-    loads[2].wait()
-    loads[3].wait()
+    loads[5].wait()
+    loads[6].wait()
     for copy in edges:
         copy.wait()
     query_block = lax.broadcasted_iota(jnp.int32, (TOK, WIDE), 0) // BLOCK
@@ -211,59 +252,64 @@
     shared.finish()
     for h in range(HEADS):
         cols = pl.ds(h * DIM, DIM)
-        glob_s[h] = dot_nt(query[:, cols], glob_keys(h)) * SCALE
+        near, glob = near_s[h], dot_nt(query[:, cols], glob_keys(h)) * SCALE
+        top = jnp.maximum(jnp.max(near, axis=1, keepdims=True), jnp.max(glob, axis=1, keepdims=True))
+        near, glob = jnp.exp(near - top), jnp.exp(glob - top)
+        near_s[h], glob_s[h] = near, glob
+        row_max[h] = jnp.broadcast_to(top, (TOK, DIM))
+        row_sum[h] = jnp.broadcast_to(
+            jnp.sum(near, axis=1, keepdims=True) + jnp.sum(glob, axis=1, keepdims=True), (TOK, DIM)
+        )
         glob_g[h] = dot_nt(grad[:, cols], glob_values(h))
     rest = pl.ds(0, SEQ - 1)
     send_to(right, slots_out.at[rest], slots.at[rest], slot_sems).wait()
 
     block_rows = [slice(j * BLOCK, (j + 1) * BLOCK) for j in range(BLOCKS)]
     picked[NPICK] = jnp.zeros((2 * BLOCK, DIM), BF16)
+
+    def far_keys(h, j):
+        return jnp.concatenate([slots[holder(h, j, p), UPPER] for p in range(PICKS)], axis=0)
+
     for h in range(HEADS):
         cols = pl.ds(h * DIM, DIM)
         q, g = query[:, cols], grad[:, cols]
-        keys = [jnp.concatenate([slots[holder(h, j, p), UPPER] for p in range(PICKS)], axis=0) for j in range(BLOCKS)]
+        keys = [far_keys(h, j) for j in range(BLOCKS)]
         values = [jnp.concatenate([slots[holder(h, j, p), LOWER] for p in range(PICKS)], axis=0) for j in range(BLOCKS)]
         far = jnp.concatenate([dot_nt(q[block_rows[j]], keys[j]) for j in range(BLOCKS)], axis=0) * SCALE
-        near, glob = near_s[h], glob_s[h]
-        row_max = jnp.maximum(
-            jnp.max(near, axis=1, keepdims=True),
-            jnp.maximum(jnp.max(far, axis=1, keepdims=True), jnp.max(glob, axis=1, keepdims=True)),
-        )
-        near, far, glob = jnp.exp(near - row_max), jnp.exp(far - row_max), jnp.exp(glob - row_max)
-        total = (
-            jnp.sum(near, axis=1, keepdims=True)
-            + jnp.sum(far, axis=1, keepdims=True)
-            + jnp.sum(glob, axis=1, keepdims=True)
-        )
-        inverse = 1.0 / total
-        near, far, glob = near * inverse, far * inverse, glob * inverse
+        old_max, old_sum = row_max[h, :, :1], row_sum[h, :, :1]
+        new_max = jnp.maximum(old_max, jnp.max(far, axis=1, keepdims=True))
+        far = jnp.exp(far - new_max)
+        shrink = jnp.exp(old_max - new_max)
+        inverse = 1.0 / (old_sum * shrink + jnp.sum(far, axis=1, keepdims=True))
+        near, far, glob = near_s[h] * (shrink * inverse), far * inverse, glob_s[h] * (shrink * inverse)
         near_b, far_b, glob_b = near.astype(BF16), far.astype(BF16), glob.astype(BF16)
         mixed = dot_nn(near_b, near_values(cols)) + dot_nn(glob_b, glob_values(h))
         mixed += jnp.concatenate([dot_nn(far_b[block_rows[j]], values[j]) for j in range(BLOCKS)], axis=0)
         attended[:, cols] = mixed.astype(BF16)
         delta = jnp.sum(g.astype(F32) * mixed, axis=1, keepdims=True)
         far_g = jnp.concatenate([dot_nt(g[block_rows[j]], values[j]) for j in range(BLOCKS)], axis=0)
-        far_d = (far * (far_g - delta)).astype(BF16)
+        far_change = (far * (far_g - delta)).astype(BF16)
+        far_d[h] = far_change
         for j in range(BLOCKS):
-            far_key = (dot_tn(far_d[block_rows[j]], q[block_rows[j]]) * SCALE).astype(BF16)
+            far_key = (dot_tn(far_change[block_rows[j]], q[block_rows[j]]) * SCALE).astype(BF16)
             far_value = dot_tn(far_b[block_rows[j]], g[block_rows[j]]).astype(BF16)
             for p in range(PICKS):
                 at = (h * BLOCKS + j) * PICKS + p
                 picked[at, UPPER] = far_key[p * BLOCK : (p + 1) * BLOCK]
                 picked[at, LOWER] = far_value[p * BLOCK : (p + 1) * BLOCK]
-        far_s[h] = jnp.concatenate([dot_nn(far_d[block_rows[j]], keys[j]) for j in range(BLOCKS)], axis=0)
         near_p[h] = near_b
         glob_p[h] = glob_b
         near_d[h] = (near * (near_g[h] - delta)).astype(BF16)
         glob_d[h] = (glob * (glob_g[h] - delta)).astype(BF16)
 
-    def return_slots(chunk):
-        @pl.loop(CHUNKS[chunk], CHUNKS[chunk + 1])
+    def return_slots(begin, end):
+        @pl.loop(begin, end)
         def _(k):
             peer = lax.rem(me + k, SEQ)
             slots_out[peer] = picked[given(peer)]
             send_to(peer, slots_out.at[peer], slots_back.at[me], slot_back_sems).start()
 
+    return_slots(CHUNKS[0], EARLY)
     for h in range(HEADS):
         cols = pl.ds(h * DIM, DIM)
         glob_key = (dot_tn(glob_d[h], query[:, cols]) * SCALE).astype(BF16)
@@ -273,7 +319,7 @@
             back_in[g, HEADS + h] = glob_value[g * TILE : (g + 1) * TILE]
     summed = Tiles(me, back_in, back_part, back_middle, back_piece, back_row, back_out, tile_back_sems)
     summed.start_first()
-    return_slots(0)
+    return_slots(EARLY, CHUNKS[1])
     slots_back[me] = picked[given(me)]
     for h in range(HEADS):
         cols = pl.ds(h * DIM, DIM)
@@ -293,14 +339,15 @@
     for copy in edges:
         copy.start()
     summed.start_second()
-    return_slots(1)
+    return_slots(CHUNKS[1], CHUNKS[2])
     summed.start_third()
-    return_slots(2)
+    return_slots(CHUNKS[2], CHUNKS[3])
     summed.start_fourth()
-    return_slots(3)
-    for h in range(HEADS):
-        cols = pl.ds(h * DIM, DIM)
-        change = dot_nn(near_d[h], near_keys(cols)) + dot_nn(glob_d[h], glob_keys(h)) + far_s[h]
+    return_slots(CHUNKS[3], CHUNKS[4])
+    for h in range(HEADS):
+        cols = pl.ds(h * DIM, DIM)
+        change = dot_nn(near_d[h], near_keys(cols)) + dot_nn(glob_d[h], glob_keys(h))
+        change += jnp.concatenate([dot_nn(far_d[h, block_rows[j]], far_keys(h, j)) for j in range(BLOCKS)], axis=0)
         grad_query[:, cols] = (change * SCALE).astype(BF16)
     summed.finish()
     tiles_back[...] = back_out[...]
@@ -309,8 +356,13 @@
     send_to(right, slots_out.at[rest], slots_back.at[rest], slot_back_sems).wait()
 
 
-def collect_kernel(tables, pos, own_key, own_value, edge, tiles, slots, grad_key, grad_value, total):
-    me = tables[2 * SEQ + NPICK]
+def collect_kernel(
+    table, pos, attended_in, query_in, own_key, own_value, edge, tiles, slots,
+    attended, grad_query, grad_key, grad_value, total,
+):
+    me = table[MINE, 0]
+    attended[...] = attended_in[...]
+    grad_query[...] = query_in[...]
     for j in range(BLOCKS):
         for h in range(HEADS):
             rows, cols = pl.ds(j * BLOCK, BLOCK), pl.ds(h * DIM, DIM)
@@ -319,7 +371,7 @@
 
     @pl.loop(0, SEQ)
     def _(k):
-        total[tables[k]] += slots[k].astype(F32)
+        total[named_by(table, k)] += slots[k].astype(F32)
 
     from_left = jnp.where(me == 0, 0.0, 1.0)
     from_right = jnp.where(me == SEQ - 1, 0.0, 1.0)
@@ -339,22 +391,11 @@
                 out[pl.ds(j * BLOCK, BLOCK), cols] = whole.astype(BF16)
 
 
-def make_tables(rand_blocks, me):
-    picks = rand_blocks.reshape(HEADS, SEQ, BLOCKS * PICKS)
-    holders = picks // BLOCKS
-    code = picks % BLOCKS * HEADS + jnp.arange(HEADS)[:, None, None]
-    want = jnp.sum(jnp.where(holders == me, code, 0), axis=(0, 2))
-    mine = lax.dynamic_slice_in_dim(holders, me, 1, 1).reshape(NPICK)
-    index = jnp.arange(NPICK)[None, :] - NPICK
-    given = NPICK + jnp.sum(jnp.where(mine[None, :] == jnp.arange(SEQ)[:, None], index, 0), axis=1)
-    return jnp.concatenate([want, given, mine, me[None]])
-
-
 def body(query_rows, key_rows, value_rows, grad_out, rand_blocks, global_pos):
-    me = lax.axis_index("seq")
     arrays = [a.reshape(TOK, COLS) for a in (query_rows, key_rows, value_rows, grad_out)]
-    tables = make_tables(rand_blocks, me)
+    names = rand_blocks.transpose(0, 3, 1, 2).reshape(PICKS, HEADS, SEQ * BLOCKS)
     pos = global_pos[None, :]
+    operands = [pltpu.with_memory_space_constraint(a, pltpu.HBM) for a in (*arrays, names, pos)]
     shape = jax.ShapeDtypeStruct
     slot_shape, edge_shape = (SEQ, 2 * BLOCK, DIM), (2, 2 * BLOCK, COLS)
     grid_shape, row_shape = (RING, RING, TILE, DIM), (RING, TILE, DIM)
@@ -363,12 +404,22 @@
     f32 = lambda dims: pltpu.VMEM(dims, F32)
     dma = pltpu.SemaphoreType.DMA
     tile_scratch = [bf16(grid_shape), bf16(grid_shape), bf16(row_shape), bf16(row_shape), bf16(row_shape), bf16(grid_shape)]
-    attended, grad_query, own_key, own_value, edge, tiles, slots = pl.pallas_call(
+    attended, grad_query, own_key, own_value, edge, tiles, slots, table = pl.pallas_call(
         main_kernel,
-        out_shape=[narrow, narrow, wide, wide, shape(edge_shape, BF16), shape(grid_shape, BF16), shape(slot_shape, BF16)],
-        in_specs=[SMEM, VMEM, ANY, ANY, ANY, ANY],
-        out_specs=[VMEM] * 7,
+        out_shape=[
+            *[narrow, narrow, wide, wide],
+            *[shape(dims, BF16) for dims in (edge_shape, grid_shape, slot_shape)],
+            shape((8, SEQ * BLOCKS), jnp.int32),
+        ],
+        in_specs=[ANY] * 6,
+        out_specs=[VMEM] * 8,
         scratch_shapes=[
+            pltpu.VMEM((PICKS, HEADS, SEQ * BLOCKS), jnp.int32),
+            pltpu.SMEM((PICKS, HEADS, SEQ * BLOCKS), jnp.int32),
+            pltpu.VMEM((1, GLOB), jnp.int32),
+            pltpu.SMEM((8, SEQ * BLOCKS), jnp.int32),
+            pltpu.VMEM((8, DIM), jnp.int32),
+            pltpu.SMEM((8, DIM), jnp.int32),
             *[bf16((TOK, COLS))] * 4,
             bf16((BLOCKS * HEADS, 2 * BLOCK, DIM)),
             bf16(slot_shape),
@@ -383,11 +434,13 @@
             bf16((HEADS, TOK, WIDE)),
             bf16((HEADS, TOK, GLOB)),
             bf16((HEADS, TOK, GLOB)),
+            bf16((HEADS, TOK, FAR)),
+            f32((HEADS, TOK, DIM)),
             f32((HEADS, TOK, DIM)),
             bf16((NPICK + 1, 2 * BLOCK, DIM)),
             bf16(edge_shape),
             *tile_scratch,
-            dma((4,)),
+            dma((9,)),
             dma((4, 2)),
             dma((4, 2)),
             dma((2,)),
@@ -399,17 +452,17 @@
             collective_id=0, has_side_effects=True, vmem_limit_bytes=48 << 20
         ),
         name="attend",
-    )(tables, pos, *arrays)
-    grad_key, grad_value = pl.pallas_call(
+    )(*operands)
+    results = pl.pallas_call(
         collect_kernel,
-        out_shape=[narrow, narrow],
-        in_specs=[SMEM] + [VMEM] * 6,
-        out_specs=[VMEM] * 2,
+        out_shape=[narrow] * 4,
+        in_specs=[SMEM] + [VMEM] * 8,
+        out_specs=[VMEM] * 4,
         scratch_shapes=[f32((BLOCKS * HEADS, 2 * BLOCK, DIM))],
         compiler_params=pltpu.CompilerParams(vmem_limit_bytes=32 << 20),
         name="collect",
-    )(tables, pos, own_key, own_value, edge, tiles, slots)
-    return tuple(a.reshape(1, TOK, COLS) for a in (attended, grad_query, grad_key, grad_value))
+    )(table, pos, attended, grad_query, own_key, own_value, edge, tiles, slots)
+    return tuple(a.reshape(1, TOK, COLS) for a in results)
 
 
 def solution(mesh):

time: 141 us -> 123 us (0.87)
  Pallas kernels: 132 us -> 122 us
  local copies, waits for them, and re-layouts: 7.15 us -> 0.65 us
    pallas_call x2, Pallas kernels: 132 us -> 122 us  [the longest x1 119 us: body(): pl.pallas_call(main_kernel, out_shape=[*[narrow, narrow, wide, wide], *[s...]
    unnamed x13 -> x2, local copies, waits for them, and re-layouts: 6.79 us -> 0.65 us
where the time goes in v3:
time: 123 us
  Pallas kernels  122 us (99%)
    pallas_call x1, Pallas kernels, body(): pl.pallas_call(main_kernel, out_shape=[*[narrow, narrow, wide, wide], *[s...  119 us
    pallas_call x1, Pallas kernels, body(): pl.pallas_call(collect_kernel, out_shape=[narrow] * 4, in_specs=[SMEM] +...  3.15 us

profile of v3, /device:TPU:1, one launch (start us, length us, event | category | flops | bytes accessed | tf_op | source)
XLA Modules:
  0.0 123.2 jit_solution(8236647599107904873)
XLA Ops:
  0.6 118.7 %attend.1 = (bf16[256,512]{1,0:T(8,128)(2,1)S(1)}, bf16[256,512]{1,0:T(8,128)(2,1)S(1)}, f32[256,512]{1,0:T(8,128)S(1)}, f32[256,512]{1,0:T(8,128)S(1)}, bf16[2,...) custom-call(bf16[256,512]{1,0:T(8,128)(2,1)} %bitcast.14, ...), custom_call_target="tpu_custom_call" | custom-call | tf_op jit(solution)/shard_map/attend/pallas_call | solution.py:407
  119.3 0.0 copy-start
  119.4 0.6 copy-done
  120.0 3.1 %collect.1 = (bf16[256,512]{1,0:T(8,128)(2,1)}, bf16[256,512]{1,0:T(8,128)(2,1)}, bf16[256,512]{1,0:T(8,128)(2,1)}, bf16[256,512]{1,0:T(8,128)(2,1)}) custom-call(s32[8,256]{1,0:T(8,128)S(1)} %get-tuple-element.16.table, s32[1,128]{1,0:T(1,128)S(1)} %bitcast.13, bf16[256,512]{1,0:T(8,128)(2,1)S(1)} %get-tuple-element.17.attended_in, ...), custom_call_target="tpu_custom_call" | custom-call | tf_op jit(solution)/shard_map/collect/pallas_call | solution.py:456
Async XLA Ops:
  119.3 0.7 copy-start

commit v4 on v3

--- a/solution.py
+++ b/solution.py
@@ -23,8 +23,8 @@
 WIDE = (BLOCKS + 2) * BLOCK
 FAR = PICKS * BLOCK
 SCALE = DIM**-0.5
-CHUNKS = (1, 21, 33, 45, SEQ)
-EARLY = 5
+CHUNKS = (1, 21, 37, 51, SEQ)
+EARLY = 9
 MINE = 1
 BF16 = jnp.bfloat16
 F32 = jnp.float32
@@ -117,7 +117,7 @@
 
 def main_kernel(
     query_hbm, key_hbm, value_hbm, grad_hbm, rand_hbm, pos_hbm,
-    attended, grad_query, own_key, own_value, edge_back, tiles_back, slots_back, table,
+    attended, grad_query, own_key, own_value, edge_back, tiles_back, slots_back, table, hot_out,
     rand, rand_smem, pos, table_smem, given_vmem, given_smem, query, key, value, grad, stacked, slots_out, slots, edge, tiles_in, part, middle, piece, row, tiles,
     near_s, near_g, glob_s, glob_g, near_p, near_d, glob_d, glob_p, far_d, row_max, row_sum, picked,
     edge_grads, back_in, back_part, back_middle, back_piece, back_row, back_out,
@@ -181,6 +181,7 @@
             stacked[j * HEADS + h, UPPER] = key[rows, cols]
             stacked[j * HEADS + h, LOWER] = value[rows, cols]
     hot = (lax.broadcasted_iota(jnp.int32, (TOK, GLOB), 0) == pos[...] - me * TOK).astype(F32).astype(BF16)
+    hot_out[...] = hot
     for c, ref in enumerate((key, value)):
         owned = dot_tn(hot, ref[...]).astype(BF16)
         for g in range(GROUPS):
@@ -357,7 +358,7 @@
 
 
 def collect_kernel(
-    table, pos, attended_in, query_in, own_key, own_value, edge, tiles, slots,
+    table, hot, attended_in, query_in, own_key, own_value, edge, tiles, slots,
     attended, grad_query, grad_key, grad_value, total,
 ):
     me = table[MINE, 0]
@@ -375,13 +376,12 @@
 
     from_left = jnp.where(me == 0, 0.0, 1.0)
     from_right = jnp.where(me == SEQ - 1, 0.0, 1.0)
-    hot = (lax.broadcasted_iota(jnp.int32, (TOK, GLOB), 0) == pos[...] - me * TOK).astype(F32).astype(BF16)
     for h in range(HEADS):
         cols = pl.ds(h * DIM, DIM)
         for c, out in enumerate((grad_key, grad_value)):
             part = pl.ds(c * BLOCK, BLOCK)
             glob = jnp.concatenate([tiles[g, c * HEADS + h] for g in range(GROUPS)], axis=0)
-            placed = dot_nn(hot, glob)
+            placed = dot_nn(hot[...], glob)
             for j in range(BLOCKS):
                 whole = total[j * HEADS + h, part] + placed[j * BLOCK : (j + 1) * BLOCK]
                 if j == 0:
@@ -404,15 +404,16 @@
     f32 = lambda dims: pltpu.VMEM(dims, F32)
     dma = pltpu.SemaphoreType.DMA
     tile_scratch = [bf16(grid_shape), bf16(grid_shape), bf16(row_shape), bf16(row_shape), bf16(row_shape), bf16(grid_shape)]
-    attended, grad_query, own_key, own_value, edge, tiles, slots, table = pl.pallas_call(
+    attended, grad_query, own_key, own_value, edge, tiles, slots, table, hot = pl.pallas_call(
         main_kernel,
         out_shape=[
             *[narrow, narrow, wide, wide],
             *[shape(dims, BF16) for dims in (edge_shape, grid_shape, slot_shape)],
             shape((8, SEQ * BLOCKS), jnp.int32),
+            shape((TOK, GLOB), BF16),
         ],
         in_specs=[ANY] * 6,
-        out_specs=[VMEM] * 8,
+        out_specs=[VMEM] * 9,
         scratch_shapes=[
             pltpu.VMEM((PICKS, HEADS, SEQ * BLOCKS), jnp.int32),
             pltpu.SMEM((PICKS, HEADS, SEQ * BLOCKS), jnp.int32),
@@ -461,7 +462,7 @@
         scratch_shapes=[f32((BLOCKS * HEADS, 2 * BLOCK, DIM))],
         compiler_params=pltpu.CompilerParams(vmem_limit_bytes=32 << 20),
         name="collect",
-    )(table, pos, attended, grad_query, own_key, own_value, edge, tiles, slots)
+    )(table, hot, attended, grad_query, own_key, own_value, edge, tiles, slots)
     return tuple(a.reshape(1, TOK, COLS) for a in results)
 
 

time: 123 us -> 120 us (0.976)
  Pallas kernels: 122 us -> 119 us
    pallas_call x1, Pallas kernels: 119 us -> 116 us  [body(): pl.pallas_call(main_kernel, out_shape=[*[narrow, narrow, wide, wide], *[s...]
where the time goes in v4:
time: 120 us
  Pallas kernels  119 us (99%)
    pallas_call x1, Pallas kernels, body(): pl.pallas_call(main_kernel, out_shape=[*[narrow, narrow, wide, wide], *[s...  116 us
    pallas_call x1, Pallas kernels, body(): pl.pallas_call(collect_kernel, out_shape=[narrow] * 4, in_specs=[SMEM] +...  3.16 us

profile of v4, /device:TPU:1, one launch (start us, length us, event | category | flops | bytes accessed | tf_op | source)
XLA Modules:
  0.0 119.9 jit_solution(9549804279273511182)
XLA Ops:
  0.6 116.1 %attend.1 = (bf16[256,512]{1,0:T(8,128)(2,1)S(1)}, bf16[256,512]{1,0:T(8,128)(2,1)S(1)}, f32[256,512]{1,0:T(8,128)S(1)}, f32[256,512]{1,0:T(8,128)S(1)}, bf16[2,...) custom-call(bf16[256,512]{1,0:T(8,128)(2,1)} %bitcast.12, ...), custom_call_target="tpu_custom_call" | custom-call | tf_op jit(solution)/shard_map/attend/pallas_call | solution.py:407
  116.7 3.2 %collect.1 = (bf16[256,512]{1,0:T(8,128)(2,1)}, bf16[256,512]{1,0:T(8,128)(2,1)}, bf16[256,512]{1,0:T(8,128)(2,1)}, bf16[256,512]{1,0:T(8,128)(2,1)}) custom-call(s32[8,256]{1,0:T(8,128)S(1)} %get-tuple-element.17.table, bf16[256,128]{1,0:T(8,128)(2,1)S(1)} %get-tuple-element.18.hot, bf16[256,512]{1,0:T(8,128)(2,1)S(1)} %get-tuple-element.19.attended_in, ...), custom_call_target="tpu_custom_call" | custom-call | tf_op jit(solution)/shard_map/collect/pallas_call | solution.py:457

commit v5 on v4

--- a/solution.py
+++ b/solution.py
@@ -117,7 +117,7 @@
 
 def main_kernel(
     query_hbm, key_hbm, value_hbm, grad_hbm, rand_hbm, pos_hbm,
-    attended, grad_query, own_key, own_value, edge_back, tiles_back, slots_back, table, hot_out,
+    attended, grad_query, own, edge_back, tiles_back, slots_back, table, hot_out,
     rand, rand_smem, pos, table_smem, given_vmem, given_smem, query, key, value, grad, stacked, slots_out, slots, edge, tiles_in, part, middle, piece, row, tiles,
     near_s, near_g, glob_s, glob_g, near_p, near_d, glob_d, glob_p, far_d, row_max, row_sum, picked,
     edge_grads, back_in, back_part, back_middle, back_piece, back_row, back_out,
@@ -327,8 +327,9 @@
         q, g = query[:, cols], grad[:, cols]
         near_key = dot_tn(near_d[h], q) * SCALE
         near_value = dot_tn(near_p[h], g)
-        own_key[:, cols] = near_key[BLOCK : BLOCK + TOK]
-        own_value[:, cols] = near_value[BLOCK : BLOCK + TOK]
+        for j in range(BLOCKS):
+            own[j * HEADS + h, UPPER] = near_key[(j + 1) * BLOCK : (j + 2) * BLOCK]
+            own[j * HEADS + h, LOWER] = near_value[(j + 1) * BLOCK : (j + 2) * BLOCK]
         edge_grads[0, UPPER, cols] = near_key[:BLOCK].astype(BF16)
         edge_grads[0, LOWER, cols] = near_value[:BLOCK].astype(BF16)
         edge_grads[1, UPPER, cols] = near_key[BLOCK + TOK :].astype(BF16)
@@ -358,17 +359,17 @@
 
 
 def collect_kernel(
-    table, hot, attended_in, query_in, own_key, own_value, edge, tiles, slots,
-    attended, grad_query, grad_key, grad_value, total,
+    table, hot, attended_in, query_in, own, edge, tiles, slots,
+    attended, grad_query, grad_key, grad_value, total, sems,
 ):
     me = table[MINE, 0]
-    attended[...] = attended_in[...]
-    grad_query[...] = query_in[...]
-    for j in range(BLOCKS):
-        for h in range(HEADS):
-            rows, cols = pl.ds(j * BLOCK, BLOCK), pl.ds(h * DIM, DIM)
-            total[j * HEADS + h, UPPER] = own_key[rows, cols]
-            total[j * HEADS + h, LOWER] = own_value[rows, cols]
+    passed = [
+        pltpu.make_async_copy(attended_in, attended, sems.at[0]),
+        pltpu.make_async_copy(query_in, grad_query, sems.at[1]),
+    ]
+    for copy in passed:
+        copy.start()
+    total[...] = own[...]
 
     @pl.loop(0, SEQ)
     def _(k):
@@ -389,6 +390,8 @@
                 if j == BLOCKS - 1:
                     whole += edge[1, part, cols].astype(F32) * from_right
                 out[pl.ds(j * BLOCK, BLOCK), cols] = whole.astype(BF16)
+    for copy in passed:
+        copy.wait()
 
 
 def body(query_rows, key_rows, value_rows, grad_out, rand_blocks, global_pos):
@@ -399,21 +402,21 @@
     shape = jax.ShapeDtypeStruct
     slot_shape, edge_shape = (SEQ, 2 * BLOCK, DIM), (2, 2 * BLOCK, COLS)
     grid_shape, row_shape = (RING, RING, TILE, DIM), (RING, TILE, DIM)
-    wide, narrow = shape((TOK, COLS), F32), shape((TOK, COLS), BF16)
+    own_shape, narrow = shape((BLOCKS * HEADS, 2 * BLOCK, DIM), F32), shape((TOK, COLS), BF16)
     bf16 = lambda dims: pltpu.VMEM(dims, BF16)
     f32 = lambda dims: pltpu.VMEM(dims, F32)
     dma = pltpu.SemaphoreType.DMA
     tile_scratch = [bf16(grid_shape), bf16(grid_shape), bf16(row_shape), bf16(row_shape), bf16(row_shape), bf16(grid_shape)]
-    attended, grad_query, own_key, own_value, edge, tiles, slots, table, hot = pl.pallas_call(
+    attended, grad_query, own, edge, tiles, slots, table, hot = pl.pallas_call(
         main_kernel,
         out_shape=[
-            *[narrow, narrow, wide, wide],
+            *[narrow, narrow, own_shape],
             *[shape(dims, BF16) for dims in (edge_shape, grid_shape, slot_shape)],
             shape((8, SEQ * BLOCKS), jnp.int32),
             shape((TOK, GLOB), BF16),
         ],
         in_specs=[ANY] * 6,
-        out_specs=[VMEM] * 9,
+        out_specs=[VMEM] * 8,
         scratch_shapes=[
             pltpu.VMEM((PICKS, HEADS, SEQ * BLOCKS), jnp.int32),
             pltpu.SMEM((PICKS, HEADS, SEQ * BLOCKS), jnp.int32),
@@ -457,12 +460,12 @@
     results = pl.pallas_call(
         collect_kernel,
         out_shape=[narrow] * 4,
-        in_specs=[SMEM] + [VMEM] * 8,
-        out_specs=[VMEM] * 4,
-        scratch_shapes=[f32((BLOCKS * HEADS, 2 * BLOCK, DIM))],
+        in_specs=[SMEM] + [VMEM] * 7,
+        out_specs=[ANY, ANY, VMEM, VMEM],
+        scratch_shapes=[f32((BLOCKS * HEADS, 2 * BLOCK, DIM)), dma((2,))],
         compiler_params=pltpu.CompilerParams(vmem_limit_bytes=32 << 20),
         name="collect",
-    )(table, hot, attended, grad_query, own_key, own_value, edge, tiles, slots)
+    )(table, hot, attended, grad_query, own, edge, tiles, slots)
     return tuple(a.reshape(1, TOK, COLS) for a in results)
 
 

time: 120 us -> 120 us (level)
  no operation moved by 1% of the time
where the time goes in v5:
time: 120 us
  Pallas kernels  119 us (99%)
    pallas_call x1, Pallas kernels, body(): pl.pallas_call(main_kernel, out_shape=[*[narrow, narrow, own_shape], *[sh...  116 us
    pallas_call x1, Pallas kernels, body(): pl.pallas_call(collect_kernel, out_shape=[narrow] * 4, in_specs=[SMEM] +...  3.14 us

profile of v5, /device:TPU:1, one launch (start us, length us, event | category | flops | bytes accessed | tf_op | source)
XLA Modules:
  0.0 119.8 jit_solution(12979744628897041000)
XLA Ops:
  0.6 116.0 %attend.1 = (bf16[256,512]{1,0:T(8,128)(2,1)S(1)}, bf16[256,512]{1,0:T(8,128)(2,1)S(1)}, f32[16,128,128]{2,1,0:T(8,128)S(1)}, bf16[2,128,512]{2,1,0:T(8,128)(2,1...) custom-call(bf16[256,512]{1,0:T(8,128)(2,1)} %bitcast.12, ...), custom_call_target="tpu_custom_call" | custom-call | tf_op jit(solution)/shard_map/attend/pallas_call | solution.py:410
  116.7 3.1 %collect.1 = (bf16[256,512]{1,0:T(8,128)(2,1)}, bf16[256,512]{1,0:T(8,128)(2,1)}, bf16[256,512]{1,0:T(8,128)(2,1)}, bf16[256,512]{1,0:T(8,128)(2,1)}) custom-call(s32[8,256]{1,0:T(8,128)S(1)} %get-tuple-element.16.table, bf16[256,128]{1,0:T(8,128)(2,1)S(1)} %get-tuple-element.17.hot, bf16[256,512]{1,0:T(8,128)(2,1)S(1)} %get-tuple-element.18.attended_in, ...), custom_call_target="tpu_custom_call" | custom-call | tf_op jit(solution)/shard_map/collect/pallas_call | solution.py:460

commit v6 on v5

--- a/solution.py
+++ b/solution.py
@@ -153,7 +153,7 @@
     asked = jnp.zeros((HEADS, SEQ * BLOCKS), jnp.int32)
     for p in range(PICKS):
         names = rand[p]
-        code = (names & (BLOCKS - 1)) * HEADS + lax.broadcasted_iota(jnp.int32, names.shape, 0)
+        code = (names & (BLOCKS - 1)) * HEADS + lax.broadcasted_iota(jnp.int32, names.shape, 0) + 1
         asked = jnp.maximum(asked, jnp.where(names >> 2 == me, code, 0))
     asked = jnp.max(asked, axis=0, keepdims=True)
     line = lax.broadcasted_iota(jnp.int32, (8, SEQ * BLOCKS), 0)
@@ -173,7 +173,7 @@
     for copy in copies:
         copy.start()
     given = lambda k: given_smem[0, k]
-    want = lambda k: named_by(table_smem, k)
+    want = lambda k: jnp.maximum(named_by(table_smem, k) - 1, 0)
 
     for j in range(BLOCKS):
         for h in range(HEADS):
@@ -373,7 +373,11 @@
 
     @pl.loop(0, SEQ)
     def _(k):
-        total[named_by(table, k)] += slots[k].astype(F32)
+        target = named_by(table, k)
+
+        @pl.when(target > 0)
+        def _():
+            total[target - 1] += slots[k].astype(F32)
 
     from_left = jnp.where(me == 0, 0.0, 1.0)
     from_right = jnp.where(me == SEQ - 1, 0.0, 1.0)

time: 120 us -> 121 us (level)
  no operation moved by 1% of the time
where the time goes in v6:
time: 121 us
  Pallas kernels  120 us (99%)
    pallas_call x1, Pallas kernels, body(): pl.pallas_call(main_kernel, out_shape=[*[narrow, narrow, own_shape], *[sh...  117 us
    pallas_call x1, Pallas kernels, body(): pl.pallas_call(collect_kernel, out_shape=[narrow] * 4, in_specs=[SMEM] +...  3.61 us

profile of v6, /device:TPU:1, one launch (start us, length us, event | category | flops | bytes accessed | tf_op | source)
XLA Modules:
  0.0 120.8 jit_solution(16824998649647863411)
XLA Ops:
  0.6 116.5 %attend.1 = (bf16[256,512]{1,0:T(8,128)(2,1)S(1)}, bf16[256,512]{1,0:T(8,128)(2,1)S(1)}, f32[16,128,128]{2,1,0:T(8,128)S(1)}, bf16[2,128,512]{2,1,0:T(8,128)(2,1...) custom-call(bf16[256,512]{1,0:T(8,128)(2,1)} %bitcast.12, ...), custom_call_target="tpu_custom_call" | custom-call | tf_op jit(solution)/shard_map/attend/pallas_call | solution.py:414
  117.2 3.6 %collect.1 = (bf16[256,512]{1,0:T(8,128)(2,1)}, bf16[256,512]{1,0:T(8,128)(2,1)}, bf16[256,512]{1,0:T(8,128)(2,1)}, bf16[256,512]{1,0:T(8,128)(2,1)}) custom-call(s32[8,256]{1,0:T(8,128)S(1)} %get-tuple-element.16.table, bf16[256,128]{1,0:T(8,128)(2,1)S(1)} %get-tuple-element.17.hot, bf16[256,512]{1,0:T(8,128)(2,1)S(1)} %get-tuple-element.18.attended_in, ...), custom_call_target="tpu_custom_call" | custom-call | tf_op jit(solution)/shard_map/collect/pallas_call | solution.py:464
